TPU v7x, 32 devices: a whole 2x2x4 slice. The times are simulated.
32 devices in a mesh: ctx: 16 (over z, y, core), fsdp: 2 (over x).
Axes of the slice: x: 2, y: 2, z: 4, core: 2. Of those that a mesh axis runs over, the one named last changes fastest.
Arguments:
- tokens: bfloat16 [2, 4096, 768], P('fsdp', 'ctx'), may hold values from -6 to 6
- lengths: int32 [2], P('fsdp'), may hold values from 1024 to 4096, as said below
- cotangent: bfloat16 [2, 4096, 768], P('fsdp', 'ctx'), may hold values from -6 to 6
- query_weight: bfloat16 [768, 768], P('ctx', 'fsdp'), may hold values from -0.21875 to 0.21875
- key_weight: bfloat16 [768, 768], P('ctx', 'fsdp'), may hold values from -0.21875 to 0.21875
- value_weight: bfloat16 [768, 768], P('ctx', 'fsdp'), may hold values from -0.21875 to 0.21875
- out_weight: bfloat16 [768, 768], P('ctx', 'fsdp'), may hold values from -6 to 6
- in_weight: bfloat16 [768, 3072], P('ctx', 'fsdp'), may hold values from -0.21875 to 0.21875
- down_weight: bfloat16 [3072, 768], P('ctx', 'fsdp'), may hold values from -0.109375 to 0.109375
- query_bias: bfloat16 [768], P('ctx'), may hold values from -3 to 3
- value_bias: bfloat16 [768], P('ctx'), may hold values from -0.119628906 to 0.119628906
- out_bias: bfloat16 [768], P('ctx'), may hold values from -3 to 3
- attn_norm_gain: bfloat16 [768], P('ctx'), may hold values from 0.5 to 1.5
- attn_norm_bias: bfloat16 [768], P('ctx'), may hold values from -2 to 2
- in_bias: bfloat16 [3072], P('ctx'), may hold values from -3 to 3
- down_bias: bfloat16 [768], P('ctx'), may hold values from -3 to 3
- ffn_norm_gain: bfloat16 [768], P('ctx'), may hold values from 0.5 to 1.5
- ffn_norm_bias: bfloat16 [768], P('ctx'), may hold values from -2 to 2
Outputs:
- layer_out: bfloat16 [2, 4096, 768], P('fsdp', 'ctx')
- tokens_grad: bfloat16 [2, 4096, 768], P('fsdp', 'ctx')
- grad_query_weight: float32 [768, 768], P('ctx', 'fsdp')
- grad_key_weight: float32 [768, 768], P('ctx', 'fsdp')
- grad_value_weight: float32 [768, 768], P('ctx', 'fsdp')
- grad_out_weight: float32 [768, 768], P('ctx', 'fsdp')
- grad_in_weight: float32 [768, 3072], P('ctx', 'fsdp')
- grad_down_weight: float32 [3072, 768], P('ctx', 'fsdp')
- grad_query_bias: float32 [768], P('ctx')
- grad_value_bias: float32 [768], P('ctx')
- grad_out_bias: float32 [768], P('ctx')
- grad_attn_norm_gain: float32 [768], P('ctx')
- grad_attn_norm_bias: float32 [768], P('ctx')
- grad_in_bias: float32 [3072], P('ctx')
- grad_down_bias: float32 [768], P('ctx')
- grad_ffn_norm_gain: float32 [768], P('ctx')
- grad_ffn_norm_bias: float32 [768], P('ctx')
- rms_values: float32 [3], replicated
Inputs may be any that keep to these rules, and one draw needn't show every extreme that they name: `lengths`: each sequence has between 1024 and 4096 valid slots; some sequence has exactly 4096, another exactly 1024.
All inputs are finite; a program needn't handle non-finite values.
Results may differ from a plain program's by a relative error of at most 0.022.
Values may be sent and summed in bfloat16 or wider, within the bound.
No kernel may reach another device: no remote copies, remote signals or barrier semaphores. Data moves between devices by JAX's collectives and lax.ppermute only.
A program may use at most 192 MiB of HBM per device.

v0:
```python
import jax
import jax.numpy as jnp
from jax import lax
from jax.sharding import PartitionSpec as P

HEAD_DIM = 64


norm_eps = 1e-12
score_scale = 0.125
masked_score = -1000000000.0
rows_contract = (((0,), (0,)), ((), ()))
columns_contract = (((1,), (1,)), ((), ()))


def layer_norm(stream, gain_vec, shift_vec):
    center = jnp.mean(stream, axis=-1, keepdims=True)
    offset = stream - center
    spread = jnp.mean(offset * offset, axis=-1, keepdims=True)
    return offset * lax.rsqrt(spread + norm_eps) * gain_vec + shift_vec


def gelu_exact(inner_pre):
    return jax.nn.gelu(inner_pre, approximate=False)


def plain_product(left_side, right_side):
    return jnp.dot(left_side, right_side, preferred_element_type=jnp.float32)


def row_product(left_side, right_side):
    return lax.dot_general(left_side, right_side, rows_contract, preferred_element_type=jnp.float32)


def column_product(left_side, right_side):
    return lax.dot_general(
        left_side, right_side, columns_contract, preferred_element_type=jnp.float32
    )


def head_scores(query_head, key_head, key_ok):
    scores = (
        jnp.einsum("sqd,skd->sqk", query_head, key_head, preferred_element_type=jnp.float32)
        * score_scale
    )
    return jnp.where(key_ok[:, None, :], scores, masked_score)


def attend(query_seq, pair_all, key_ok):
    seq_count, slot_count, model_width = query_seq.shape
    heads_count = model_width // HEAD_DIM

    def one_head(head_index, loop_state):
        mixed_out, log_totals = loop_state
        head_start = head_index * HEAD_DIM
        query_head = lax.dynamic_slice_in_dim(query_seq, head_start, HEAD_DIM, 2)
        key_head = lax.dynamic_slice_in_dim(pair_all, head_start, HEAD_DIM, 2)
        value_head = lax.dynamic_slice_in_dim(pair_all, model_width + head_start, HEAD_DIM, 2)
        scores = head_scores(query_head, key_head, key_ok)
        row_peak = jnp.max(scores, axis=-1, keepdims=True)
        row_expo = jnp.exp(scores - row_peak)
        row_total = jnp.sum(row_expo, axis=-1, keepdims=True)
        attn_probs = (row_expo / row_total).astype(jnp.bfloat16)
        head_out = jnp.einsum(
            "sqk,skd->sqd", attn_probs, value_head, preferred_element_type=jnp.float32
        )
        mixed_out = lax.dynamic_update_slice_in_dim(mixed_out, head_out, head_start, 2)
        log_row = row_peak[..., 0] + jnp.log(row_total[..., 0])
        log_totals = lax.dynamic_update_index_in_dim(log_totals, log_row, head_index, 0)
        return (mixed_out, log_totals)

    start_state = (
        jnp.zeros((seq_count, slot_count, model_width), jnp.float32),
        jnp.zeros((heads_count, seq_count, slot_count), jnp.float32),
    )
    return lax.fori_loop(0, heads_count, one_head, start_state)


def attend_back(query_seq, pair_all, key_ok, log_totals, grad_mixed):
    seq_count, slot_count, model_width = query_seq.shape
    heads_count = model_width // HEAD_DIM

    def one_head(head_index, loop_state):
        grad_query, grad_pair = loop_state
        head_start = head_index * HEAD_DIM
        query_head = lax.dynamic_slice_in_dim(query_seq, head_start, HEAD_DIM, 2)
        key_head = lax.dynamic_slice_in_dim(pair_all, head_start, HEAD_DIM, 2)
        value_head = lax.dynamic_slice_in_dim(pair_all, model_width + head_start, HEAD_DIM, 2)
        grad_head = lax.dynamic_slice_in_dim(grad_mixed, head_start, HEAD_DIM, 2)
        scores = head_scores(query_head, key_head, key_ok)
        log_row = lax.dynamic_index_in_dim(log_totals, head_index, 0, keepdims=False)
        attn_probs = jnp.exp(scores - log_row[..., None])
        probs_b = attn_probs.astype(jnp.bfloat16)
        grad_probs = jnp.einsum(
            "sqd,skd->sqk", grad_head, value_head, preferred_element_type=jnp.float32
        )
        row_inner = jnp.sum(attn_probs * grad_probs, axis=-1, keepdims=True)
        grad_scores = (attn_probs * (grad_probs - row_inner)).astype(jnp.bfloat16)
        grad_query_head = (
            jnp.einsum("sqk,skd->sqd", grad_scores, key_head, preferred_element_type=jnp.float32)
            * score_scale
        )
        grad_key_head = (
            jnp.einsum("sqk,sqd->skd", grad_scores, query_head, preferred_element_type=jnp.float32)
            * score_scale
        )
        grad_value_head = jnp.einsum(
            "sqk,sqd->skd", probs_b, grad_head, preferred_element_type=jnp.float32
        )
        grad_query = lax.dynamic_update_slice_in_dim(grad_query, grad_query_head, head_start, 2)
        grad_pair = lax.dynamic_update_slice_in_dim(grad_pair, grad_key_head, head_start, 2)
        grad_pair = lax.dynamic_update_slice_in_dim(
            grad_pair, grad_value_head, model_width + head_start, 2
        )
        return (grad_query, grad_pair)

    start_state = (jnp.zeros(query_seq.shape, jnp.float32), jnp.zeros(pair_all.shape, jnp.float32))
    return lax.fori_loop(0, heads_count, one_head, start_state)


def column_sums(matrix_b):
    return jnp.sum(matrix_b.astype(jnp.float32), axis=0)


def body(
    tokens,
    lengths,
    cotangent,
    query_weight,
    key_weight,
    value_weight,
    out_weight,
    in_weight,
    down_weight,
    query_bias,
    value_bias,
    out_bias,
    attn_norm_gain,
    attn_norm_bias,
    in_bias,
    down_bias,
    ffn_norm_gain,
    ffn_norm_bias,
):
    seq_count, slot_count, model_width = tokens.shape
    row_count = seq_count * slot_count
    ctx_size = lax.axis_size("ctx")
    ctx_index = lax.axis_index("ctx")
    row_parts = (
        lax.all_gather(query_weight, "ctx", axis=0, tiled=True),
        lax.all_gather(key_weight, "ctx", axis=0, tiled=True),
        lax.all_gather(value_weight, "ctx", axis=0, tiled=True),
        lax.all_gather(out_weight, "ctx", axis=0, tiled=True),
        lax.all_gather(in_weight, "ctx", axis=0, tiled=True),
        lax.all_gather(down_weight, "ctx", axis=0, tiled=True),
        lax.all_gather(query_bias, "ctx", axis=0, tiled=True),
        lax.all_gather(value_bias, "ctx", axis=0, tiled=True),
        lax.all_gather(out_bias, "ctx", axis=0, tiled=True),
        lax.all_gather(attn_norm_gain, "ctx", axis=0, tiled=True),
        lax.all_gather(attn_norm_bias, "ctx", axis=0, tiled=True),
        lax.all_gather(in_bias, "ctx", axis=0, tiled=True),
        lax.all_gather(down_bias, "ctx", axis=0, tiled=True),
        lax.all_gather(ffn_norm_gain, "ctx", axis=0, tiled=True),
        lax.all_gather(ffn_norm_bias, "ctx", axis=0, tiled=True),
    )
    full_mats = (
        lax.all_gather(row_parts[0], "fsdp", axis=1, tiled=True),
        lax.all_gather(row_parts[1], "fsdp", axis=1, tiled=True),
        lax.all_gather(row_parts[2], "fsdp", axis=1, tiled=True),
        lax.all_gather(row_parts[3], "fsdp", axis=1, tiled=True),
        lax.all_gather(row_parts[4], "fsdp", axis=1, tiled=True),
        lax.all_gather(row_parts[5], "fsdp", axis=1, tiled=True),
    )
    query_full, key_full, value_full, out_full, in_full, down_full = full_mats
    query_vec = row_parts[6].astype(jnp.float32)
    value_vec = row_parts[7].astype(jnp.float32)
    out_vec = row_parts[8].astype(jnp.float32)
    gain_one = row_parts[9].astype(jnp.float32)
    bias_one = row_parts[10].astype(jnp.float32)
    in_vec = row_parts[11].astype(jnp.float32)
    down_vec = row_parts[12].astype(jnp.float32)
    gain_two = row_parts[13].astype(jnp.float32)
    bias_two = row_parts[14].astype(jnp.float32)
    local_slots = ctx_index * slot_count + jnp.arange(slot_count)
    local_ok = local_slots[None, :] < lengths[:, None]
    valid_mask = local_ok.astype(jnp.float32)
    valid_col = valid_mask.reshape(row_count, 1)
    key_ok = jnp.arange(slot_count * ctx_size)[None, :] < lengths[:, None]
    token_rows = tokens.reshape(row_count, model_width)
    queries_b = (plain_product(token_rows, query_full) + query_vec).astype(jnp.bfloat16)
    keys_b = plain_product(token_rows, key_full).astype(jnp.bfloat16)
    values_b = (plain_product(token_rows, value_full) + value_vec).astype(jnp.bfloat16)
    pair_local = jnp.concatenate([keys_b, values_b], axis=1).reshape(
        seq_count, slot_count, 2 * model_width
    )
    pair_all = lax.all_gather(pair_local, "ctx", axis=1, tiled=True)
    query_seq = queries_b.reshape(seq_count, slot_count, model_width)
    mixed_out, log_totals = attend(query_seq, pair_all, key_ok)
    mixed_b = mixed_out.reshape(row_count, model_width).astype(jnp.bfloat16)
    attn_branch = plain_product(mixed_b, out_full) + out_vec
    stream = token_rows.astype(jnp.float32) + attn_branch
    norm_one, norm_one_back = jax.vjp(layer_norm, stream, gain_one, bias_one)
    norm_one_b = norm_one.astype(jnp.bfloat16)
    inner_pre = plain_product(norm_one_b, in_full) + in_vec
    act_out, gelu_back = jax.vjp(gelu_exact, inner_pre)
    act_b = act_out.astype(jnp.bfloat16)
    ffn_branch = plain_product(act_b, down_full) + down_vec
    stream_two = norm_one + ffn_branch
    final_out, norm_two_back = jax.vjp(layer_norm, stream_two, gain_two, bias_two)
    layer_out = (
        (valid_col * final_out).astype(jnp.bfloat16).reshape(seq_count, slot_count, model_width)
    )
    grad_final = valid_col * cotangent.reshape(row_count, model_width).astype(jnp.float32)
    grad_stream_two, grad_gain_two, grad_bias_two = norm_two_back(grad_final)
    grad_ffn_b = grad_stream_two.astype(jnp.bfloat16)
    grad_down_vec = column_sums(grad_ffn_b)
    grad_down_full = row_product(act_b, grad_ffn_b)
    grad_inner_b = gelu_back(column_product(grad_ffn_b, down_full))[0].astype(jnp.bfloat16)
    grad_in_vec = column_sums(grad_inner_b)
    grad_in_full = row_product(norm_one_b, grad_inner_b)
    grad_norm_one = grad_stream_two + column_product(grad_inner_b, in_full)
    grad_stream, grad_gain_one, grad_bias_one = norm_one_back(grad_norm_one)
    grad_attn_b = grad_stream.astype(jnp.bfloat16)
    grad_out_vec = column_sums(grad_attn_b)
    grad_out_full = row_product(mixed_b, grad_attn_b)
    grad_mixed = (
        column_product(grad_attn_b, out_full)
        .astype(jnp.bfloat16)
        .reshape(seq_count, slot_count, model_width)
    )
    grad_query_seq, grad_pair = attend_back(query_seq, pair_all, key_ok, log_totals, grad_mixed)
    grad_pair_local = lax.psum_scatter(
        grad_pair.astype(jnp.bfloat16), "ctx", scatter_dimension=1, tiled=True
    ).astype(jnp.float32)
    grad_keys_b = (
        grad_pair_local[:, :, :model_width].reshape(row_count, model_width).astype(jnp.bfloat16)
    )
    grad_values_b = (
        grad_pair_local[:, :, model_width:].reshape(row_count, model_width).astype(jnp.bfloat16)
    )
    grad_queries_b = grad_query_seq.reshape(row_count, model_width).astype(jnp.bfloat16)
    grad_query_full = row_product(token_rows, grad_queries_b)
    grad_query_vec = column_sums(grad_queries_b)
    grad_key_full = row_product(token_rows, grad_keys_b)
    grad_value_full = row_product(token_rows, grad_values_b)
    grad_value_vec = column_sums(grad_values_b)
    tokens_grad = (
        (
            grad_stream
            + column_product(grad_queries_b, query_full)
            + column_product(grad_keys_b, key_full)
            + column_product(grad_values_b, value_full)
        )
        .astype(jnp.bfloat16)
        .reshape(seq_count, slot_count, model_width)
    )
    narrow = (
        lax.psum_scatter(
            grad_query_full.astype(jnp.bfloat16), "fsdp", scatter_dimension=1, tiled=True
        ).astype(jnp.float32),
        lax.psum_scatter(
            grad_key_full.astype(jnp.bfloat16), "fsdp", scatter_dimension=1, tiled=True
        ).astype(jnp.float32),
        lax.psum_scatter(
            grad_value_full.astype(jnp.bfloat16), "fsdp", scatter_dimension=1, tiled=True
        ).astype(jnp.float32),
        lax.psum_scatter(
            grad_out_full.astype(jnp.bfloat16), "fsdp", scatter_dimension=1, tiled=True
        ).astype(jnp.float32),
        lax.psum_scatter(
            grad_in_full.astype(jnp.bfloat16), "fsdp", scatter_dimension=1, tiled=True
        ).astype(jnp.float32),
        lax.psum_scatter(
            grad_down_full.astype(jnp.bfloat16), "fsdp", scatter_dimension=1, tiled=True
        ).astype(jnp.float32),
    )
    owned_grads = (
        lax.psum_scatter(
            narrow[0].astype(jnp.bfloat16), "ctx", scatter_dimension=0, tiled=True
        ).astype(jnp.float32),
        lax.psum_scatter(
            narrow[1].astype(jnp.bfloat16), "ctx", scatter_dimension=0, tiled=True
        ).astype(jnp.float32),
        lax.psum_scatter(
            narrow[2].astype(jnp.bfloat16), "ctx", scatter_dimension=0, tiled=True
        ).astype(jnp.float32),
        lax.psum_scatter(
            narrow[3].astype(jnp.bfloat16), "ctx", scatter_dimension=0, tiled=True
        ).astype(jnp.float32),
        lax.psum_scatter(
            narrow[4].astype(jnp.bfloat16), "ctx", scatter_dimension=0, tiled=True
        ).astype(jnp.float32),
        lax.psum_scatter(
            narrow[5].astype(jnp.bfloat16), "ctx", scatter_dimension=0, tiled=True
        ).astype(jnp.float32),
    )
    moments = jnp.stack(
        [
            jnp.sum(valid_col * stream * stream),
            jnp.sum(valid_col * attn_branch * attn_branch),
            jnp.sum(valid_col * ffn_branch * ffn_branch),
            jnp.sum(valid_col),
        ]
    )
    summed = lax.psum(
        (
            moments,
            grad_query_vec,
            grad_value_vec,
            grad_out_vec,
            grad_gain_one,
            grad_bias_one,
            grad_in_vec,
            grad_down_vec,
            grad_gain_two,
            grad_bias_two,
        ),
        ("ctx", "fsdp"),
    )
    width_shard = query_bias.shape[0]
    hidden_shard = in_bias.shape[0]

    def own_piece(vector_full, shard_len):
        return lax.dynamic_slice_in_dim(vector_full, ctx_index * shard_len, shard_len, 0)

    rms_values = jnp.sqrt(summed[0][:3] / (summed[0][3] * model_width))
    return (
        layer_out,
        tokens_grad,
        owned_grads[0],
        owned_grads[1],
        owned_grads[2],
        owned_grads[3],
        owned_grads[4],
        owned_grads[5],
        own_piece(summed[1], width_shard),
        own_piece(summed[2], width_shard),
        own_piece(summed[3], width_shard),
        own_piece(summed[4], width_shard),
        own_piece(summed[5], width_shard),
        own_piece(summed[6], hidden_shard),
        own_piece(summed[7], width_shard),
        own_piece(summed[8], width_shard),
        own_piece(summed[9], width_shard),
        rms_values,
    )


def solution(mesh):
    in_specs = (
        P("fsdp", "ctx", None),
        P("fsdp"),
        P("fsdp", "ctx", None),
        P("ctx", "fsdp"),
        P("ctx", "fsdp"),
        P("ctx", "fsdp"),
        P("ctx", "fsdp"),
        P("ctx", "fsdp"),
        P("ctx", "fsdp"),
        P("ctx"),
        P("ctx"),
        P("ctx"),
        P("ctx"),
        P("ctx"),
        P("ctx"),
        P("ctx"),
        P("ctx"),
        P("ctx"),
    )
    out_specs = (
        P("fsdp", "ctx", None),
        P("fsdp", "ctx", None),
        P("ctx", "fsdp"),
        P("ctx", "fsdp"),
        P("ctx", "fsdp"),
        P("ctx", "fsdp"),
        P("ctx", "fsdp"),
        P("ctx", "fsdp"),
        P("ctx"),
        P("ctx"),
        P("ctx"),
        P("ctx"),
        P("ctx"),
        P("ctx"),
        P("ctx"),
        P("ctx"),
        P("ctx"),
        P(),
    )
    return jax.shard_map(body, mesh=mesh, in_specs=in_specs, out_specs=out_specs, check_vma=False)
```

profile of v0, /device:TPU:0, one launch (start us, length us, event | category | flops | bytes accessed | tf_op | source)
XLA Modules:
  0.0 1333.7 jit_solution(6212013291559108767)
XLA Ops:
  7.4 26.6 %all_gather.69 = bf16[768,384]{1,0:T(8,128)(2,1)} all-gather(bf16[48,384]{1,0:T(8,128)(2,1)} %param.26), channel_id=1, replica_groups=mesh['ctx'=16,'fsdp'=2] {'ctx'}, dimensions={0}, use_global_device_ids=true | all-gather | bytes 626688 | tf_op jit(solution)/shard_map/all_gather | solution.py:151
  34.1 20.7 %all_gather.71 = bf16[768,384]{1,0:T(8,128)(2,1)} all-gather(bf16[48,384]{1,0:T(8,128)(2,1)} %param.27), channel_id=1, replica_groups=mesh['ctx'=16,'fsdp'=2] {'ctx'}, dimensions={0}, use_global_device_ids=true | all-gather | bytes 626688 | tf_op jit(solution)/shard_map/all_gather | solution.py:152
  55.6 22.2 %all_gather.66 = bf16[768,384]{1,0:T(8,128)(2,1)} all-gather(bf16[48,384]{1,0:T(8,128)(2,1)} %param.25), channel_id=1, replica_groups=mesh['ctx'=16,'fsdp'=2] {'ctx'}, dimensions={0}, use_global_device_ids=true | all-gather | bytes 626688 | tf_op jit(solution)/shard_map/all_gather | solution.py:150
  82.5 58.1 %all-reduce.10 = (bf16[768]{0:T(1024)(128)(2,1)S(1)}, bf16[768]{0:T(1024)(128)(2,1)S(1)}, bf16[3072]{0:T(1024)(128)(2,1)S(1)}, bf16[768]{0:T(1024)(128)(2,1)S(1)...) all-reduce(bf16[768]{0:T(1024)(128)(2,1)S(1)} %dynamic-update-slice, ...), channel_id=1, replica_groups=mesh['ctx'=16,'fsdp'=2] {'ctx'}, use_global_device_ids=true, to_apply=%add | all-reduce | flops 9216 | bytes 36864
  145.2 20.6 %all_gather.75 = bf16[768,384]{1,0:T(8,128)(2,1)} all-gather(bf16[48,384]{1,0:T(8,128)(2,1)S(1)} %copy-done.13), channel_id=1, replica_groups=mesh['ctx'=16,'fsdp'=2] {'ctx'}, dimensions={0}, use_global_device_ids=true | all-gather | bytes 626688 | tf_op jit(solution)/shard_map/all_gather | solution.py:153
  169.1 21.9 %all-gather.23.cloned.1.call-done = bf16[3072,384]{1,0:T(8,128)(2,1)} async-done(((bf16[192,384]{1,0:T(8,128)(2,1)}), bf16[3072,384]{1,0:T(8,128)(2,1)}) %all-gather.23.cloned.1.call-update) | async-done | bytes 2359312 | tf_op jit(solution)/shard_map/all_gather | solution.py:155
  191.6 101.1 %all-gather.27.cloned.1.call-done = bf16[4096,1536]{1,0:T(8,128)(2,1)} async-done(((bf16[256,1536]{1,0:T(8,128)(2,1)}), bf16[4096,1536]{1,0:T(8,128)(2,1)}) %all-gather.27.cloned.1.call-update) | async-done | bytes 12582928 | tf_op jit(solution)/shard_map/all_gather | solution.py:196
  292.8 77.5 %while.36 = (s32[]{:T(128)}, bf16[1,256,768]{1,2,0:T(8,128)(2,1)S(1)}, f32[12,1,256]{2,1,0:T(1,128)S(1)}, bf16[1,256,768]{2,1,0:T(8,128)(2,1)S(1)}, bf16[1,4096,...) while((s32[]{:T(128)}, ...), condition=%wide.region_3.4_spmd.clone, body=%wide.region_0.3_spmd.clone.sunk | while | flops 276827904 | bytes 14829822 | solution.py:76
  372.6 7.0 all-gather.21.cloned.1.call-done
  379.5 11.7 multiply_convert_fusion.1
  391.3 52.5 %all-gather.25.cloned.1.call-done = bf16[3072,768]{1,0:T(8,128)(2,1)} async-done(((bf16[3072,384]{1,0:T(8,128)(2,1)}), bf16[3072,768]{1,0:T(8,128)(2,1)}) %all-gather.25.cloned.1.call-update) | async-done | bytes 4718608 | tf_op jit(solution)/shard_map/all_gather | solution.py:172
  443.8 4.5 fusion.101
  458.8 6.1 broadcast_in_dim.102
  464.8 142.3 %while.37 = (s32[]{:T(128)}, bf16[1,256,768]{1,2,0:T(8,128)(2,1)S(1)}, bf16[1,4096,1536]{1,2,0:T(8,128)(2,1)}, bf16[1,256,768]{2,1,0:T(8,128)(2,1)S(1)}, bf16[1,...) while((s32[]{:T(128)}, ...), condition=%wide.region_14.15_spmd.clone, body=%wide.region_12.14_spmd.clone.sunk | while | flops 680808192 | bytes 37041444 | solution.py:118
  611.9 5.7 convolution_convert_fusion.1
  619.5 3.7 convolution_convert_fusion
  623.2 7.1 copy.50
  630.4 111.7 %reduce-scatter.24.cloned.1.call-done = bf16[1,256,1536]{1,2,0:T(8,128)(2,1)} async-done(((bf16[1,4096,1536]{1,2,0:T(8,128)(2,1)}), bf16[1,256,1536]{1,2,0:T(8,128)(2,1)}) %reduce-scatter.24.cloned.1.call-update) | async-done | bytes 786448 | tf_op jit(solution)/shard_map/reduce_scatter | solution.py:232
  744.6 20.6 %reduce-scatter.26.cloned.1.call-done = bf16[768,384]{0,1:T(8,128)(2,1)} async-done(((bf16[768,768]{0,1:T(8,128)(2,1)}), bf16[768,384]{0,1:T(8,128)(2,1)}) %reduce-scatter.26.cloned.1.call-update) | async-done | bytes 589840 | tf_op jit(solution)/shard_map/reduce_scatter | solution.py:258
  767.4 21.8 %reduce-scatter.46.cloned.1.call-done = bf16[384,768]{1,0:T(8,128)(2,1)} async-done(((bf16[768,768]{1,0:T(8,128)(2,1)}), bf16[384,768]{1,0:T(8,128)(2,1)}) %reduce-scatter.46.cloned.1.call-update) | async-done | bytes 589840
  791.4 60.1 %reduce-scatter.34.cloned.1.call-done = bf16[768,1536]{1,0:T(8,128)(2,1)} async-done(((bf16[768,3072]{1,0:T(8,128)(2,1)}), bf16[768,1536]{1,0:T(8,128)(2,1)}) %reduce-scatter.34.cloned.1.call-update) | async-done | bytes 2359312 | tf_op jit(solution)/shard_map/reduce_scatter | solution.py:270
  851.6 62.2 %reduce-scatter.48.cloned.1.call-done = bf16[384,3072]{1,0:T(8,128)(2,1)} async-done(((bf16[768,3072]{1,0:T(8,128)(2,1)}), bf16[384,3072]{1,0:T(8,128)(2,1)}) %reduce-scatter.48.cloned.1.call-update) | async-done | bytes 2359312
  913.8 4.4 copy.51
  919.9 17.8 %reduce-scatter.28.cloned.1.call-done = bf16[768,384]{0,1:T(8,128)(2,1)} async-done(((bf16[768,768]{0,1:T(8,128)(2,1)}), bf16[768,384]{0,1:T(8,128)(2,1)}) %reduce-scatter.28.cloned.1.call-update) | async-done | bytes 589840 | tf_op jit(solution)/shard_map/reduce_scatter | solution.py:261
  946.5 49.9 %reduce-scatter.40.cloned.1.call-done = bf16[48,384]{1,0:T(8,128)(2,1)} async-done(((bf16[768,384]{1,0:T(8,128)(2,1)}), bf16[48,384]{1,0:T(8,128)(2,1)}) %reduce-scatter.40.cloned.1.call-update) | async-done | bytes 36880
  998.0 55.6 %reduce-scatter.32.cloned.1.call-done = bf16[48,384]{1,0:T(8,128)(2,1)} async-done(((bf16[768,384]{1,0:T(8,128)(2,1)}), bf16[48,384]{1,0:T(8,128)(2,1)}) %reduce-scatter.32.cloned.1.call-update) | async-done | bytes 36880 | tf_op jit(solution)/shard_map/reduce_scatter | solution.py:287
  1055.1 64.7 %reduce-scatter.36.cloned.1.call-done = bf16[48,1536]{1,0:T(8,128)(2,1)} async-done(((bf16[768,1536]{1,0:T(8,128)(2,1)}), bf16[48,1536]{1,0:T(8,128)(2,1)}) %reduce-scatter.36.cloned.1.call-update) | async-done | bytes 147472 | tf_op jit(solution)/shard_map/reduce_scatter | solution.py:290
  1121.4 64.2 %reduce-scatter.38.cloned.1.call-done = bf16[192,384]{1,0:T(8,128)(2,1)} async-done(((bf16[3072,384]{1,0:T(8,128)(2,1)}), bf16[192,384]{1,0:T(8,128)(2,1)}) %reduce-scatter.38.cloned.1.call-update) | async-done | bytes 147472 | tf_op jit(solution)/shard_map/reduce_scatter | solution.py:293
  1187.3 21.4 %reduce-scatter.30.cloned.1.call-done = bf16[768,384]{0,1:T(8,128)(2,1)} async-done(((bf16[768,768]{0,1:T(8,128)(2,1)}), bf16[768,384]{0,1:T(8,128)(2,1)}) %reduce-scatter.30.cloned.1.call-update) | async-done | bytes 589840 | tf_op jit(solution)/shard_map/reduce_scatter | solution.py:264
  1211.0 40.4 %all-reduce.9 = (f32[768]{0:T(1024)S(1)}, f32[768]{0:T(1024)S(1)}, f32[768]{0:T(1024)S(1)}, f32[768]{0:T(1024)S(1)}, f32[768]{0:T(1024)S(1)}, /*index=5*/f32[307...) all-reduce(f32[768]{0:T(1024)S(1)} %convert_reduce_fusion.4, ...), channel_id=1, replica_groups=mesh['ctx'=16,'fsdp'=2] {'ctx','fsdp'}, use_global_device_ids=true, to_apply=%region_29.30 | all-reduce | flops 9220 | bytes 73760 | tf_op jit(solution)/shard_map/psum | solution.py:305
  1260.4 6.8 reduce-scatter.42.cloned.1.call-done
  1268.8 56.3 %reduce-scatter.44.cloned.1.call-done = bf16[48,384]{1,0:T(8,128)(2,1)} async-done(((bf16[768,384]{1,0:T(8,128)(2,1)}), bf16[48,384]{1,0:T(8,128)(2,1)}) %reduce-scatter.44.cloned.1.call-update) | async-done | bytes 36880
  (383 shorter events, 287.4 us)
Async XLA Ops:
  7.3 133.3 %copy-start = (bf16[1,256,768]{2,1,0:T(8,128)(2,1)S(1)}, bf16[1,256,768]{2,1,0:T(8,128)(2,1)}, u32[]{:S(2)}) copy-start(bf16[1,256,768]{2,1,0:T(8,128)(2,1)} %param.22) | copy-start | bytes 1179652
  7.3 133.3 %all-gather.13.cloned.1.call-start = ((), (), s32[]{:S(2)}) async-start(), calls=%async_computation.14 | async-start | bytes 1769472 | tf_op jit(solution)/shard_map/all_gather | solution.py:168
  34.0 108.4 %all-gather.15.cloned.1.call-start = ((), (), s32[]{:S(2)}) async-start(), calls=%async_computation.15 | async-start | bytes 1769472 | tf_op jit(solution)/shard_map/all_gather | solution.py:169
  54.8 111.1 %all-gather.19.cloned.1.call-start = ((), (), s32[]{:S(2)}) async-start(), calls=%async_computation.17 | async-start | bytes 2506752 | tf_op jit(solution)/shard_map/all_gather | solution.py:154
  55.5 111.9 %all-gather.11.cloned.1.call-start = ((), (), s32[]{:S(2)}) async-start(), calls=%async_computation.13 | async-start | bytes 1769472 | tf_op jit(solution)/shard_map/all_gather | solution.py:167
  77.8 113.3 %all-gather.23.cloned.1.call-start = ((), (), s32[]{:S(2)}) async-start(), calls=%async_computation.19 | async-start | bytes 2506752 | tf_op jit(solution)/shard_map/all_gather | solution.py:155
  78.4 214.4 %all-gather.27.cloned.1.call-start = ((), (), s32[]{:S(2)}) async-start(), calls=%async_computation.29 | async-start | bytes 13369344 | tf_op jit(solution)/shard_map/all_gather | solution.py:196
  145.1 225.2 %all-gather.17.cloned.1.call-start = ((), (), s32[]{:S(2)}) async-start(), calls=%async_computation.16 | async-start | bytes 1769472 | tf_op jit(solution)/shard_map/all_gather | solution.py:170
  165.8 213.7 %all-gather.21.cloned.1.call-start = ((), (), s32[]{:S(2)}) async-start(), calls=%async_computation.18 | async-start | bytes 7077888 | tf_op jit(solution)/shard_map/all_gather | solution.py:171
  166.5 277.2 %all-gather.25.cloned.1.call-start = ((), (), s32[]{:S(2)}) async-start(), calls=%async_computation.20 | async-start | bytes 7077888 | tf_op jit(solution)/shard_map/all_gather | solution.py:172
  191.1 551.0 %reduce-scatter.24.cloned.1.call-start = ((), (), s32[]{:S(2)}) async-start(), calls=%async_computation.21 | async-start | bytes 13369344 | tf_op jit(solution)/shard_map/reduce_scatter | solution.py:232
  372.6 84.3 %copy-start.17 = (f32[256]{0:T(256)}, f32[256]{0:T(256)S(1)}, u32[]{:S(2)}) copy-start(f32[256]{0:T(256)S(1)} %fusion.90) | copy-start | bytes 3076
  607.2 158.1 %reduce-scatter.26.cloned.1.call-start = ((), (), s32[]{:S(2)}) async-start(), calls=%async_computation.22 | async-start | bytes 1769472 | tf_op jit(solution)/shard_map/reduce_scatter | solution.py:258
  608.8 180.4 %reduce-scatter.46.cloned.1.call-start = ((), (), s32[]{:S(2)}) async-start(), calls=%async_computation.33 | async-start | bytes 1769472
  611.9 239.6 %reduce-scatter.34.cloned.1.call-start = ((), (), s32[]{:S(2)}) async-start(), calls=%async_computation.26 | async-start | bytes 7077888 | tf_op jit(solution)/shard_map/reduce_scatter | solution.py:270
  617.7 296.1 %reduce-scatter.48.cloned.1.call-start = ((), (), s32[]{:S(2)}) async-start(), calls=%async_computation.34 | async-start | bytes 7077888
  630.3 307.4 %reduce-scatter.28.cloned.1.call-start = ((), (), s32[]{:S(2)}) async-start(), calls=%async_computation.23 | async-start | bytes 1769472 | tf_op jit(solution)/shard_map/reduce_scatter | solution.py:261
  744.6 251.9 %reduce-scatter.40.cloned.1.call-start = ((), (), s32[]{:S(2)}) async-start(), calls=%async_computation.30 | async-start | bytes 626688
  767.4 286.3 %reduce-scatter.32.cloned.1.call-start = ((), (), s32[]{:S(2)}) async-start(), calls=%async_computation.25 | async-start | bytes 626688 | tf_op jit(solution)/shard_map/reduce_scatter | solution.py:287
  791.4 328.4 %reduce-scatter.36.cloned.1.call-start = ((), (), s32[]{:S(2)}) async-start(), calls=%async_computation.27 | async-start | bytes 2506752 | tf_op jit(solution)/shard_map/reduce_scatter | solution.py:290
  851.5 334.1 %reduce-scatter.38.cloned.1.call-start = ((), (), s32[]{:S(2)}) async-start(), calls=%async_computation.28 | async-start | bytes 2506752 | tf_op jit(solution)/shard_map/reduce_scatter | solution.py:293
  918.2 290.4 %reduce-scatter.30.cloned.1.call-start = ((), (), s32[]{:S(2)}) async-start(), calls=%async_computation.24 | async-start | bytes 1769472 | tf_op jit(solution)/shard_map/reduce_scatter | solution.py:264
  919.8 347.4 %reduce-scatter.42.cloned.1.call-start = ((), (), s32[]{:S(2)}) async-start(), calls=%async_computation.31 | async-start | bytes 626688
  939.9 385.2 %reduce-scatter.44.cloned.1.call-start = ((), (), s32[]{:S(2)}) async-start(), calls=%async_computation.32 | async-start | bytes 626688
  943.6 267.4 %copy-start.14 = (f32[768]{0:T(1024)S(1)}, f32[768]{0:T(1024)}, u32[]{:S(2)}) copy-start(f32[768]{0:T(1024)} %get-tuple-element.457) | copy-start | bytes 9220
  943.6 267.4 %copy-start.15 = (f32[768]{0:T(1024)S(1)}, f32[768]{0:T(1024)}, u32[]{:S(2)}) copy-start(f32[768]{0:T(1024)} %get-tuple-element.505) | copy-start | bytes 9220
  943.6 267.4 %copy-start.16 = (f32[768]{0:T(1024)S(1)}, f32[768]{0:T(1024)}, u32[]{:S(2)}) copy-start(f32[768]{0:T(1024)} %get-tuple-element.509) | copy-start | bytes 9220
  943.7 267.4 %copy-start.18 = (f32[3072]{0:T(1024)S(1)}, f32[3072]{0:T(1024)}, u32[]{:S(2)}) copy-start(f32[3072]{0:T(1024)} %get-tuple-element.507) | copy-start | bytes 36868
  943.7 267.4 %copy-start.20 = (f32[768]{0:T(1024)S(1)}, f32[768]{0:T(1024)}, u32[]{:S(2)}) copy-start(f32[768]{0:T(1024)} %get-tuple-element.446) | copy-start | bytes 9220
  943.7 267.4 %copy-start.21 = (f32[768]{0:T(1024)S(1)}, f32[768]{0:T(1024)}, u32[]{:S(2)}) copy-start(f32[768]{0:T(1024)} %get-tuple-element.451) | copy-start | bytes 9220
  943.7 314.9 %copy-start.2 = (bf16[768,768]{1,0:T(8,128)(2,1)S(1)}, bf16[768,768]{1,0:T(8,128)(2,1)}, u32[]{:S(2)}) copy-start(bf16[768,768]{1,0:T(8,128)(2,1)} %all-gather.13.cloned.1.call-done) | copy-start | bytes 3538948
  946.5 312.0 %copy-start.7 = (f32[256,768]{1,0:T(8,128)S(1)}, f32[256,768]{1,0:T(8,128)}, u32[]{:S(2)}) copy-start(f32[256,768]{1,0:T(8,128)} %convolution_add_fusion.3) | copy-start | bytes 2359300
  (27 other events, 816.9 us)
Sparse Core Ops, SparseCore 0:
  34.1 20.0 all-gather.12
  55.8 22.7 all-gather.14
  80.9 42.4 all-gather.18
  124.7 21.5 all-gather.10
  148.5 42.5 all-gather.22
  193.2 99.5 all-gather.26
  294.3 20.9 all-gather.16
  316.8 62.6 all-gather.20
  381.1 62.6 all-gather.24
  607.3 134.7 reduce-scatter.23
  744.3 20.8 reduce-scatter.25
  767.4 21.7 reduce-scatter.45
  791.5 59.9 reduce-scatter.33
  853.8 59.9 reduce-scatter.47
  915.9 21.7 reduce-scatter.27
  941.5 54.8 reduce-scatter.39
  999.8 53.7 reduce-scatter.31
  1057.7 62.0 reduce-scatter.35
  1123.6 62.0 reduce-scatter.37
  1187.8 20.7 reduce-scatter.29
  1212.2 54.9 reduce-scatter.41
  1271.1 53.8 reduce-scatter.43
where the time goes:
time: 1340 us; the launch traced here: 1330 us
  waiting for transfers between devices  798 us (60%)
  matrix products  232 us (17%)
  blocking collectives  189 us (14%)
  other arithmetic  51.6 us (4%)
  local copies, waits for them, and re-layouts  43.3 us (3%)
  between operations  17.9 us (1%)
    unnamed x27, waiting for transfers between devices  199 us
    reduce_scatter x1, waiting for transfers between devices, body(): lax.psum_scatter(grad_pair.astype(jnp.bfloat16), 'ctx', scatter_dimension...  112 us
    all_gather x1, waiting for transfers between devices, body(): pair_all = lax.all_gather(pair_local, 'ctx', axis=1, tiled=True)  101 us
    reduce_scatter x1, waiting for transfers between devices, body(): lax.psum_scatter(narrow[4].astype(jnp.bfloat16), 'ctx', scatter_dimension...  64.7 us
    reduce_scatter x1, waiting for transfers between devices, body(): lax.psum_scatter(narrow[5].astype(jnp.bfloat16), 'ctx', scatter_dimension...  64.2 us
    reduce_scatter x1, waiting for transfers between devices, body(): lax.psum_scatter(grad_in_full.astype(jnp.bfloat16), 'fsdp', scatter_dimen...  60.1 us
    dot_general x24, matrix products, head_scores(): jnp.einsum('sqd,skd->sqk', query_head, key_head, preferred_element_type=j...  59.8 us
    unnamed x1, blocking collectives  58.1 us
  transfers between devices with their start and end apart: 22, of which 17 were waited for; matrix products, arithmetic and copies ran while one was open for 12% of the time, Pallas kernels for 0%

commit v1 on v0

--- a/solution.py
+++ b/solution.py
@@ -1,6 +1,10 @@
+import functools
+
 import jax
 import jax.numpy as jnp
 from jax import lax
+from jax.experimental import pallas as pl
+from jax.experimental.pallas import tpu as pltpu
 from jax.sharding import PartitionSpec as P
 
 HEAD_DIM = 64
@@ -346,6 +350,570 @@
     )
 
 
+HEADS_HERE = 3
+HEAD_COLS = HEADS_HERE * HEAD_DIM
+rows_first = (((0,), (0,)), ((), ()))
+lanes_both = (((1,), (1,)), ((), ()))
+plain_contract = (((1,), (0,)), ((), ()))
+kernel_params = pltpu.CompilerParams(vmem_limit_bytes=40 * 1024 * 1024)
+
+
+def product32(left_side, right_side, contract):
+    return lax.dot_general(left_side, right_side, contract, preferred_element_type=jnp.float32)
+
+
+def ctx_move(value, mask, levels=None):
+    pairs = [(i, i ^ mask) for i in range(16) if levels is None or (i >> 2) in levels]
+    return lax.ppermute(value, "ctx", pairs)
+
+
+def core_swap(value):
+    return ctx_move(value, 1)
+
+
+def y_swap(value):
+    return ctx_move(value, 2)
+
+
+def x_swap(value):
+    return lax.ppermute(value, "fsdp", [(0, 1), (1, 0)])
+
+
+def add_b(left_side, right_side):
+    return (left_side.astype(jnp.float32) + right_side.astype(jnp.float32)).astype(jnp.bfloat16)
+
+
+MIDDLE, ENDS = (1, 2), (0, 3)
+
+
+def z_gather(block, at_end):
+    one = ctx_move(block, 4)
+    across = ctx_move(block, 12, MIDDLE)
+    two_end = ctx_move(across, 4, MIDDLE)
+    two_mid = ctx_move(one, 12, MIDDLE)
+    three_end = ctx_move(two_mid, 4, MIDDLE)
+    return one, jnp.where(at_end, two_end, two_mid), jnp.where(at_end, three_end, across)
+
+
+def z_reduce(own, one, two, three):
+    two_sum = add_b(two, ctx_move(three, 4, ENDS))
+    three_sum = add_b(three, ctx_move(two, 4, ENDS))
+    one_sum = add_b(one, ctx_move(two_sum, 12, MIDDLE))
+    own_sum = add_b(own, ctx_move(three_sum, 12, MIDDLE))
+    return add_b(own_sum, ctx_move(one_sum, 4))
+
+
+def when_flag(flag_ref, run, idle):
+    if flag_ref is None:
+        run()
+    else:
+        pl.when(flag_ref[0] > 0)(run)
+        pl.when(flag_ref[0] <= 0)(idle)
+
+
+def attend_kernel(count, first, last, flagged, *refs):
+    flag_ref = refs[0] if flagged else None
+    refs = refs[flagged:]
+    query_ref, pairs = refs[0], refs[1 : 1 + count]
+    refs = refs[1 + count :]
+    if not first:
+        peak_in, total_in, mixed_in = refs[:3]
+        refs = refs[3:]
+
+    def one_head(head, carry):
+        key_rows = pl.ds(pl.multiple_of(head * HEAD_DIM, HEAD_DIM), HEAD_DIM)
+        value_rows = pl.ds(pl.multiple_of(HEAD_COLS + head * HEAD_DIM, HEAD_DIM), HEAD_DIM)
+        query = query_ref[key_rows, :]
+        width = query.shape[1]
+        if first:
+            peak = jnp.full((1, width), -1e30, jnp.float32)
+            total = jnp.zeros((1, width), jnp.float32)
+            mixed = jnp.zeros((HEAD_DIM, width), jnp.float32)
+        else:
+            peak, total, mixed = peak_in[head][0:1], total_in[head][0:1], mixed_in[key_rows, :]
+        for pair in pairs:
+            scores = product32(pair[key_rows, :], query, rows_first)
+            new_peak = jnp.maximum(peak, jnp.max(scores, axis=0, keepdims=True))
+            expo = jnp.exp(scores - new_peak)
+            shrink = jnp.exp(peak - new_peak)
+            total = total * shrink + jnp.sum(expo, axis=0, keepdims=True)
+            mixed = mixed * shrink + product32(
+                pair[value_rows, :], expo.astype(jnp.bfloat16), plain_contract
+            )
+            peak = new_peak
+        if last:
+            mixed_out, log_out = refs
+            mixed_out[key_rows, :] = (mixed / total).astype(jnp.bfloat16)
+            log_out[head] = jnp.broadcast_to(peak + jnp.log(total), (8, width))
+        else:
+            peak_out, total_out, sum_out = refs
+            peak_out[head] = jnp.broadcast_to(peak, (8, width))
+            total_out[head] = jnp.broadcast_to(total, (8, width))
+            sum_out[key_rows, :] = mixed
+        return carry
+
+    def run():
+        lax.fori_loop(0, HEADS_HERE, one_head, 0)
+
+    def idle():
+        for ref in refs:
+            ref[...] = jnp.zeros_like(ref)
+
+    when_flag(flag_ref, run, idle)
+
+
+def attend_call(query, pairs, state=None, last=False, flag=None):
+    width = query.shape[1]
+    stat = jax.ShapeDtypeStruct((HEADS_HERE, 8, width), jnp.float32)
+    if last:
+        outs = [jax.ShapeDtypeStruct((HEAD_COLS, width), jnp.bfloat16), stat]
+    else:
+        outs = [stat, stat, jax.ShapeDtypeStruct((HEAD_COLS, width), jnp.float32)]
+    ins = [query, *pairs, *(() if state is None else state)]
+    specs = [pl.BlockSpec(memory_space=pltpu.VMEM)] * len(ins)
+    if flag is not None:
+        ins, specs = [flag, *ins], [pl.BlockSpec(memory_space=pltpu.SMEM), *specs]
+    return pl.pallas_call(
+        functools.partial(attend_kernel, len(pairs), state is None, last, int(flag is not None)),
+        out_shape=outs,
+        in_specs=specs,
+        compiler_params=kernel_params,
+    )(*ins)
+
+
+def attend_back_kernel(count, first, flagged, *refs):
+    flag_ref = refs[0] if flagged else None
+    refs = refs[flagged:]
+    query_ref, grad_ref, log_ref, inner_ref = refs[:4]
+    pairs = refs[4 : 4 + count]
+    refs = refs[4 + count :]
+    if not first:
+        grad_query_in, refs = refs[0], refs[1:]
+    grad_query_out, grad_pairs = refs[0], refs[1:]
+
+    def one_head(head, carry):
+        key_rows = pl.ds(pl.multiple_of(head * HEAD_DIM, HEAD_DIM), HEAD_DIM)
+        value_rows = pl.ds(pl.multiple_of(HEAD_COLS + head * HEAD_DIM, HEAD_DIM), HEAD_DIM)
+        query, grad = query_ref[key_rows, :], grad_ref[key_rows, :]
+        log_row, inner = log_ref[head][0:1], inner_ref[head][0:1]
+        if first:
+            grad_query = jnp.zeros((HEAD_DIM, query.shape[1]), jnp.float32)
+        else:
+            grad_query = grad_query_in[key_rows, :]
+        for pair, grad_pair in zip(pairs, grad_pairs):
+            keys = pair[key_rows, :]
+            probs = jnp.exp(product32(keys, query, rows_first) - log_row)
+            grad_probs = product32(pair[value_rows, :], grad, rows_first)
+            grad_scores = (probs * (grad_probs - inner)).astype(jnp.bfloat16)
+            grad_query = grad_query + product32(keys, grad_scores, plain_contract)
+            grad_pair[key_rows, :] = product32(query, grad_scores, lanes_both).astype(jnp.bfloat16)
+            grad_pair[value_rows, :] = product32(
+                grad, probs.astype(jnp.bfloat16), lanes_both
+            ).astype(jnp.bfloat16)
+        grad_query_out[key_rows, :] = grad_query
+        return carry
+
+    def run():
+        lax.fori_loop(0, HEADS_HERE, one_head, 0)
+
+    def idle():
+        for ref in refs:
+            ref[...] = jnp.zeros_like(ref)
+
+    when_flag(flag_ref, run, idle)
+
+
+def attend_back_call(query, grad, log_rows, inner, pairs, grad_query=None, flag=None):
+    outs = [jax.ShapeDtypeStruct(query.shape, jnp.float32)]
+    outs += [jax.ShapeDtypeStruct(pair.shape, jnp.bfloat16) for pair in pairs]
+    ins = [query, grad, log_rows, inner, *pairs, *(() if grad_query is None else (grad_query,))]
+    specs = [pl.BlockSpec(memory_space=pltpu.VMEM)] * len(ins)
+    if flag is not None:
+        ins, specs = [flag, *ins], [pl.BlockSpec(memory_space=pltpu.SMEM), *specs]
+    return pl.pallas_call(
+        functools.partial(
+            attend_back_kernel, len(pairs), grad_query is None, int(flag is not None)
+        ),
+        out_shape=outs,
+        in_specs=specs,
+        compiler_params=kernel_params,
+    )(*ins)
+
+
+def place_kernel(count, me_ref, *refs):
+    blocks, (mats_ref, vecs_ref, sem) = refs[:count], refs[count:]
+    me = me_ref[0]
+    copies = []
+    for slot, block in enumerate(blocks):
+        core, z = slot // 4, slot % 4
+        for y in range(2):
+            owner = jnp.bitwise_xor(me, z * 4 + y * 2 + core)
+            n = (slot * 2 + y) * 2
+            copies.append(
+                pltpu.make_async_copy(block.at[y, pl.ds(0, 48)], mats_ref.at[owner], sem.at[n])
+            )
+            copies.append(
+                pltpu.make_async_copy(block.at[y, pl.ds(48, 8)], vecs_ref.at[owner], sem.at[n + 1])
+            )
+    for copy in copies:
+        copy.start()
+    for copy in copies:
+        copy.wait()
+
+
+def place_blocks(me, blocks):
+    width = blocks[0].shape[-1]
+    return pl.pallas_call(
+        functools.partial(place_kernel, len(blocks)),
+        out_shape=[
+            jax.ShapeDtypeStruct((16, 48, width), jnp.bfloat16),
+            jax.ShapeDtypeStruct((16, 8, width), jnp.bfloat16),
+        ],
+        in_specs=[pl.BlockSpec(memory_space=pltpu.SMEM)]
+        + [pl.BlockSpec(memory_space=pl.ANY)] * len(blocks),
+        out_specs=[pl.BlockSpec(memory_space=pl.ANY)] * 2,
+        scratch_shapes=[pltpu.SemaphoreType.DMA((len(blocks) * 4,))],
+    )(me, *blocks)
+
+
+def all_sum(packed):
+    for mask in (1, 2, 4, 8):
+        packed = packed + ctx_move(packed, mask)
+    return packed + x_swap(packed)
+
+
+def fast_body(
+    tokens,
+    lengths,
+    cotangent,
+    query_weight,
+    key_weight,
+    value_weight,
+    out_weight,
+    in_weight,
+    down_weight,
+    query_bias,
+    value_bias,
+    out_bias,
+    attn_norm_gain,
+    attn_norm_bias,
+    in_bias,
+    down_bias,
+    ffn_norm_gain,
+    ffn_norm_bias,
+):
+    slot_count, width = tokens.shape[1:]
+    me = lax.axis_index("ctx")
+    x_at = lax.axis_index("fsdp")
+    z_at, y_at, core_at = me >> 2, (me >> 1) & 1, me & 1
+    at_end = (z_at == 0) | (z_at == 3)
+    y_low, x_low, core_low = y_at == 0, x_at == 0, core_at == 0
+    own_long = lengths[0] == slot_count * lax.axis_size("ctx")
+    short_flag = (z_at == 0).astype(jnp.int32).reshape(1)
+
+    out_all = lax.all_gather(out_weight, ("fsdp", "ctx"), axis=0, tiled=True).reshape(2, 768, 384)
+    in_all = lax.all_gather(in_weight, ("fsdp", "ctx"), axis=0, tiled=True).reshape(2, 768, 1536)
+    down_all = lax.all_gather(down_weight, ("fsdp", "ctx"), axis=0, tiled=True).reshape(
+        2, 3072, 384
+    )
+
+    half = HEAD_COLS
+    low_cols = jnp.concatenate(
+        [query_weight[:, :half], key_weight[:, :half], value_weight[:, :half]], axis=1
+    )
+    high_cols = jnp.concatenate(
+        [query_weight[:, half:], key_weight[:, half:], value_weight[:, half:]], axis=1
+    )
+    vectors = jnp.concatenate(
+        [
+            query_bias,
+            value_bias,
+            out_bias,
+            attn_norm_gain,
+            attn_norm_bias,
+            in_bias,
+            down_bias,
+            ffn_norm_gain,
+            ffn_norm_bias,
+        ]
+    )
+    vector_rows = jnp.broadcast_to(vectors[None, :], (8, 576))
+    keep_cols = jnp.concatenate([jnp.where(y_low, low_cols, high_cols), vector_rows], axis=0)
+    send_cols = jnp.concatenate([jnp.where(y_low, high_cols, low_cols), vector_rows], axis=0)
+    own_block = jnp.stack([keep_cols, y_swap(send_cols)])
+    z_blocks = [own_block] + [ctx_move(own_block, mask) for mask in (4, 8, 12)]
+    blocks = z_blocks + [core_swap(block) for block in z_blocks]
+    qkv_weight, vecs = place_blocks(me.reshape(1), blocks)
+    qkv_weight = qkv_weight.reshape(768, 576)
+    vecs = vecs[:, 0, :].astype(jnp.float32)
+
+    def vector(start, count):
+        return vecs[:, start : start + count].reshape(16 * count)
+
+    query_vec, value_vec, out_vec = vector(0, 48), vector(48, 48), vector(96, 48)
+    gain_one, bias_one = vector(144, 48), vector(192, 48)
+    in_vec = vector(240, 192)
+    down_vec, gain_two, bias_two = vector(432, 48), vector(480, 48), vector(528, 48)
+    head_start = 384 * x_at + half * y_at
+    query_add = lax.dynamic_slice_in_dim(query_vec, head_start, half, 0)[:, None]
+    value_add = lax.dynamic_slice_in_dim(value_vec, head_start, half, 0)[:, None]
+    pair_add = jnp.concatenate([jnp.zeros_like(value_add), value_add], axis=0)
+
+    token_rows = tokens[0]
+    other_rows = x_swap(token_rows)
+    long_own = jnp.where(own_long, token_rows, other_rows)
+    short_own = jnp.where(own_long, other_rows, token_rows)
+    long_rows = jnp.concatenate([long_own, y_swap(long_own)], axis=0)
+    short_rows = jnp.concatenate([short_own, y_swap(short_own)], axis=0)
+
+    def project(rows):
+        query = product32(qkv_weight[:, :half], rows, (((0,), (1,)), ((), ()))) + query_add
+        pair = product32(qkv_weight[:, half:], rows, (((0,), (1,)), ((), ()))) + pair_add
+        scale = jnp.asarray(score_scale, jnp.bfloat16)
+        return query.astype(jnp.bfloat16) * scale, pair.astype(jnp.bfloat16)
+
+    long_query, long_pair = project(long_rows)
+    short_query, short_pair = project(short_rows)
+    z_pairs = (long_pair, *z_gather(long_pair, at_end))
+    pairs = [(pair, core_swap(pair)) for pair in z_pairs]
+    short_pairs = (short_pair, core_swap(short_pair))
+    short_mixed, short_log = attend_call(short_query, short_pairs, last=True, flag=short_flag)
+    state = None
+    for step, both in enumerate(pairs):
+        state = attend_call(long_query, both, state, last=step == 3)
+    long_mixed, long_log = state
+
+    rows_here = slot_count
+    sent = jnp.concatenate([long_mixed[:, rows_here:], short_mixed[:, rows_here:]], axis=0)
+    got = y_swap(sent)
+
+    def by_y(mine, theirs):
+        return jnp.concatenate(
+            [jnp.where(y_low, mine, theirs), jnp.where(y_low, theirs, mine)], axis=0
+        )
+
+    long_heads = by_y(long_mixed[:, :rows_here], got[:half])
+    short_heads = by_y(short_mixed[:, :rows_here], got[half:])
+    own_heads = jnp.where(own_long, long_heads, short_heads)
+    far_heads = x_swap(jnp.where(own_long, short_heads, long_heads))
+    mixed_t = jnp.concatenate(
+        [jnp.where(x_low, own_heads, far_heads), jnp.where(x_low, far_heads, own_heads)], axis=0
+    )
+
+    local_slots = me * slot_count + jnp.arange(slot_count)
+    valid_col = (local_slots < lengths[0]).astype(jnp.float32)[:, None]
+    attn_branch = (
+        jnp.concatenate([product32(mixed_t, out_all[i], rows_first) for i in range(2)], axis=1)
+        + out_vec
+    )
+    stream = token_rows.astype(jnp.float32) + attn_branch
+    norm_one, norm_one_back = jax.vjp(layer_norm, stream, gain_one, bias_one)
+    norm_one_b = norm_one.astype(jnp.bfloat16)
+    inner_pre = [
+        plain_product(norm_one_b, in_all[i]) + in_vec[1536 * i : 1536 * (i + 1)] for i in range(2)
+    ]
+    act_b, gelu_backs = [], []
+    for part in inner_pre:
+        act_out, gelu_back = jax.vjp(gelu_exact, part)
+        act_b.append(act_out.astype(jnp.bfloat16))
+        gelu_backs.append(gelu_back)
+    act_all = jnp.concatenate(act_b, axis=1)
+    ffn_branch = (
+        jnp.concatenate([plain_product(act_all, down_all[i]) for i in range(2)], axis=1) + down_vec
+    )
+    stream_two = norm_one + ffn_branch
+    final_out, norm_two_back = jax.vjp(layer_norm, stream_two, gain_two, bias_two)
+    layer_out = (valid_col * final_out).astype(jnp.bfloat16)[None]
+    grad_final = valid_col * cotangent[0].astype(jnp.float32)
+    grad_stream_two, grad_gain_two, grad_bias_two = norm_two_back(grad_final)
+    grad_ffn_b = grad_stream_two.astype(jnp.bfloat16)
+    grad_down_vec = column_sums(grad_ffn_b)
+    grad_down = jnp.concatenate(
+        [row_product(act_all, grad_ffn_b[:, 384 * i : 384 * (i + 1)]) for i in range(2)], axis=0
+    ).astype(jnp.bfloat16)
+    grad_act = sum(
+        column_product(grad_ffn_b[:, 384 * i : 384 * (i + 1)], down_all[i]) for i in range(2)
+    )
+    grad_inner_b = [
+        gelu_backs[i](grad_act[:, 1536 * i : 1536 * (i + 1)])[0].astype(jnp.bfloat16)
+        for i in range(2)
+    ]
+    grad_in_vec = jnp.concatenate([column_sums(part) for part in grad_inner_b])
+    grad_in = jnp.concatenate([row_product(norm_one_b, part) for part in grad_inner_b], axis=0)
+    grad_in = grad_in.astype(jnp.bfloat16)
+    grad_norm_one = grad_stream_two + sum(
+        column_product(grad_inner_b[i], in_all[i]) for i in range(2)
+    )
+    grad_stream, grad_gain_one, grad_bias_one = norm_one_back(grad_norm_one)
+    grad_attn_b = grad_stream.astype(jnp.bfloat16)
+    grad_out_vec = column_sums(grad_attn_b)
+    grad_out = jnp.concatenate(
+        [plain_product(mixed_t, grad_attn_b[:, 384 * i : 384 * (i + 1)]) for i in range(2)], axis=0
+    ).astype(jnp.bfloat16)
+    grad_mixed_t = sum(
+        product32(out_all[i], grad_attn_b[:, 384 * i : 384 * (i + 1)], lanes_both)
+        for i in range(2)
+    ).astype(jnp.bfloat16)
+
+    owned_out = lax.psum_scatter(grad_out, ("fsdp", "ctx"), scatter_dimension=0, tiled=True)
+    owned_in = lax.psum_scatter(grad_in, ("fsdp", "ctx"), scatter_dimension=0, tiled=True)
+    owned_down = lax.psum_scatter(grad_down, ("fsdp", "ctx"), scatter_dimension=0, tiled=True)
+
+    keep_x = jnp.where(x_low, grad_mixed_t[:384], grad_mixed_t[384:])
+    got_x = x_swap(jnp.where(x_low, grad_mixed_t[384:], grad_mixed_t[:384]))
+    long_x = jnp.where(own_long, keep_x, got_x)
+    short_x = jnp.where(own_long, got_x, keep_x)
+    both_keep = jnp.where(y_low, long_x[:half], long_x[half:])
+    short_keep = jnp.where(y_low, short_x[:half], short_x[half:])
+    sent = jnp.concatenate(
+        [
+            jnp.where(y_low, long_x[half:], long_x[:half]),
+            jnp.where(y_low, short_x[half:], short_x[:half]),
+        ],
+        axis=0,
+    )
+    got = y_swap(sent)
+    long_grad = jnp.concatenate([both_keep, got[:half]], axis=1)
+    short_grad = jnp.concatenate([short_keep, got[half:]], axis=1)
+
+    def inner_rows(mixed, grad):
+        product = mixed.astype(jnp.float32) * grad.astype(jnp.float32)
+        sums = jnp.sum(product.reshape(HEADS_HERE, HEAD_DIM, -1), axis=1, keepdims=True)
+        return jnp.broadcast_to(sums, (HEADS_HERE, 8, sums.shape[-1]))
+
+    short_back = attend_back_call(
+        short_query,
+        short_grad,
+        short_log,
+        inner_rows(short_mixed, short_grad),
+        short_pairs,
+        flag=short_flag,
+    )
+    long_inner = inner_rows(long_mixed, long_grad)
+    grad_query, reduced = None, [None] * 4
+    for step in (3, 2, 1, 0):
+        grad_query, near, far = attend_back_call(
+            long_query, long_grad, long_log, long_inner, pairs[step], grad_query
+        )
+        reduced[step] = add_b(near, core_swap(far))
+    long_pair_grad = z_reduce(*reduced)
+    short_pair_grad = add_b(short_back[1], core_swap(short_back[2]))
+    long_all = jnp.concatenate(
+        [(grad_query * score_scale).astype(jnp.bfloat16), long_pair_grad], axis=0
+    )
+    short_all = jnp.concatenate(
+        [(short_back[0] * score_scale).astype(jnp.bfloat16), short_pair_grad], axis=0
+    )
+
+    grad_qkv = product32(long_rows, long_all, (((0,), (1,)), ((), ()))) + product32(
+        short_rows, short_all, (((0,), (1,)), ((), ()))
+    )
+    grad_qkv = grad_qkv.astype(jnp.bfloat16).reshape(4, 2, 2, 48, 576)
+    core_keep = jnp.where(core_low, grad_qkv[:, :, 0], grad_qkv[:, :, 1])
+    core_send = jnp.where(core_low, grad_qkv[:, :, 1], grad_qkv[:, :, 0])
+    core_sum = add_b(core_keep, core_swap(core_send))
+    own_sum = lax.dynamic_index_in_dim(core_sum, z_at, 0, keepdims=False).astype(jnp.float32)
+    for mask in (1, 2, 3):
+        piece = lax.dynamic_index_in_dim(core_sum, z_at ^ mask, 0, keepdims=False)
+        own_sum = own_sum + ctx_move(piece, 4 * mask).astype(jnp.float32)
+    y_keep = jnp.where(y_low, own_sum[0], own_sum[1])
+    y_got = y_swap(jnp.where(y_low, own_sum[1], own_sum[0]).astype(jnp.bfloat16))
+    y_got = y_got.astype(jnp.float32)
+    low_part, high_part = jnp.where(y_low, y_keep, y_got), jnp.where(y_low, y_got, y_keep)
+    owned_qkv = [
+        jnp.concatenate(
+            [low_part[:, half * i : half * (i + 1)], high_part[:, half * i : half * (i + 1)]],
+            axis=1,
+        )
+        for i in range(3)
+    ]
+
+    def back_rows(grads):
+        return product32(grads, qkv_weight, (((0,), (1,)), ((), ())))
+
+    long_back, short_rows_back = back_rows(long_all), back_rows(short_all)
+    sent = jnp.concatenate([long_back[rows_here:], short_rows_back[rows_here:]], axis=0)
+    got = y_swap(sent.astype(jnp.bfloat16)).astype(jnp.float32)
+    long_part = long_back[:rows_here] + got[:rows_here]
+    short_part = short_rows_back[:rows_here] + got[rows_here:]
+    own_part = jnp.where(own_long, long_part, short_part)
+    far_part = x_swap(jnp.where(own_long, short_part, long_part).astype(jnp.bfloat16))
+    tokens_grad = (grad_stream + own_part + far_part.astype(jnp.float32)).astype(jnp.bfloat16)
+
+    moments = jnp.stack(
+        [
+            jnp.sum(valid_col * stream * stream),
+            jnp.sum(valid_col * attn_branch * attn_branch),
+            jnp.sum(valid_col * ffn_branch * ffn_branch),
+            jnp.sum(valid_col),
+        ]
+    )
+    packed = jnp.concatenate(
+        [
+            grad_out_vec,
+            grad_gain_one,
+            grad_bias_one,
+            grad_in_vec,
+            grad_down_vec,
+            grad_gain_two,
+            grad_bias_two,
+            moments,
+            jnp.zeros((508,), jnp.float32),
+        ]
+    )
+    summed = all_sum(packed.reshape(64, 128)).reshape(8192)
+
+    def lane_sums(first_part, second_part):
+        return jnp.sum(first_part.astype(jnp.float32), axis=1) + jnp.sum(
+            second_part.astype(jnp.float32), axis=1
+        )
+
+    query_sums = lane_sums(long_all[:half], short_all[:half])
+    value_sums = lane_sums(long_all[2 * half :], short_all[2 * half :])
+    at_heads = (jnp.arange(4) == 2 * x_at + y_at).astype(jnp.float32)[:, None]
+    head_sums = jnp.concatenate(
+        [
+            (at_heads * query_sums[None, :]).reshape(6, 128),
+            (at_heads * value_sums[None, :]).reshape(6, 128),
+            jnp.zeros((4, 128), jnp.float32),
+        ],
+        axis=0,
+    )
+    head_sums = all_sum(head_sums).reshape(2048)
+
+    def own_piece(vector_all, start, shard):
+        return lax.dynamic_slice_in_dim(vector_all, start + me * shard, shard, 0)
+
+    rms_values = jnp.sqrt(summed[7680:7683] / (summed[7683] * width))
+    return (
+        layer_out,
+        tokens_grad[None],
+        owned_qkv[0],
+        owned_qkv[1],
+        owned_qkv[2],
+        owned_out.astype(jnp.float32),
+        owned_in.astype(jnp.float32),
+        owned_down.astype(jnp.float32),
+        own_piece(head_sums, 0, 48),
+        own_piece(head_sums, 768, 48),
+        own_piece(summed, 0, 48),
+        own_piece(summed, 768, 48),
+        own_piece(summed, 1536, 48),
+        own_piece(summed, 2304, 192),
+        own_piece(summed, 5376, 48),
+        own_piece(summed, 6144, 48),
+        own_piece(summed, 6912, 48),
+        rms_values,
+    )
+
+
+def layer_body(tokens, *others):
+    fits = lax.axis_size("ctx") == 16 and lax.axis_size("fsdp") == 2
+    if fits and tokens.shape == (1, 256, 768):
+        return fast_body(tokens, *others)
+    return body(tokens, *others)
+
+
 def solution(mesh):
     in_specs = (
         P("fsdp", "ctx", None),
@@ -387,4 +955,4 @@
         P("ctx"),
         P(),
     )
-    return jax.shard_map(body, mesh=mesh, in_specs=in_specs, out_specs=out_specs, check_vma=False)
+    return jax.shard_map(layer_body, mesh=mesh, in_specs=in_specs, out_specs=out_specs, check_vma=False)

time: 1340 us -> 571 us (0.43)
  waiting for transfers between devices: 798 us -> 279 us
  matrix products: 232 us -> 42.5 us
  blocking collectives: 189 us -> 0 us
  Pallas kernels: 0 us -> 79.8 us
  starting transfers between devices: 1.68 us -> 56.4 us
    reduce_scatter x8 -> x3, waiting for transfers between devices: 416 us -> 153 us  [the longest x1 111 us: fast_body(): lax.psum_scatter(grad_down, ('fsdp', 'ctx'), scatter_dimension=0, tiled=T...]
    unnamed x27 -> x6, waiting for transfers between devices: 199 us -> 2.11 us
    all_gather x9 -> x3, waiting for transfers between devices: 183 us -> 9.09 us  [the longest x1 9.09 us: fast_body(): lax.all_gather(down_weight, ('fsdp', 'ctx'), axis=0, tiled=True)]
    dot_general x84 -> x12, matrix products: 182 us -> 12.1 us  [product32(): lax.dot_general(left_side, right_side, contract, preferred_element_type=j...]
    ppermute x0 -> x52, waiting for transfers between devices: none -> 114 us  [the longest x46 102 us: ctx_move(): return lax.ppermute(value, 'ctx', pairs)]
    all_gather x4 -> x0, blocking collectives: 90.1 us -> none  [the longest x1 26.6 us: body(): lax.all_gather(key_weight, 'ctx', axis=0, tiled=True)]
    pallas_call x0 -> x11, Pallas kernels: none -> 79.8 us  [the longest x1 36.1 us: place_blocks(): pl.pallas_call(functools.partial(place_kernel, len(blocks)), out_shape=[j...]
    unnamed x1 -> x0, blocking collectives: 58.1 us -> none
  transfers between devices with their start and end apart: 22 -> 58, of which waited for: 17 -> 25; matrix products, arithmetic and copies ran while one was open for 12% -> 17% of each run, Pallas kernels for 0% -> 14%
where the time goes in v1:
time: 571 us; the launch traced here: 564 us
  waiting for transfers between devices  279 us (49%)
  Pallas kernels  79.8 us (14%)
  starting transfers between devices  56.4 us (10%)
  other arithmetic  48.8 us (9%)
  matrix products  42.5 us (7%)
  local copies, waits for them, and re-layouts  40.8 us (7%)
  between operations  17.5 us (3%)
    reduce_scatter x1, waiting for transfers between devices, fast_body(): lax.psum_scatter(grad_down, ('fsdp', 'ctx'), scatter_dimension=0, tiled=T...  111 us
    ppermute x46, waiting for transfers between devices, ctx_move(): return lax.ppermute(value, 'ctx', pairs)  102 us
    ppermute x46, starting transfers between devices, ctx_move(): return lax.ppermute(value, 'ctx', pairs)  47.3 us
    reduce_scatter x1, waiting for transfers between devices, fast_body(): lax.psum_scatter(grad_in, ('fsdp', 'ctx'), scatter_dimension=0, tiled=True)  42.3 us
    pallas_call x1, Pallas kernels, place_blocks(): pl.pallas_call(functools.partial(place_kernel, len(blocks)), out_shape=[j...  36.1 us
    pallas_call x5, Pallas kernels, attend_back_call(): pl.pallas_call(functools.partial(attend_back_kernel, len(pairs), grad_que...  26.1 us
    dot_general x6, matrix products, plain_product(): return jnp.dot(left_side, right_side, preferred_element_type=jnp.float32)  18.1 us
    pallas_call x5, Pallas kernels, attend_call(): pl.pallas_call(functools.partial(attend_kernel, len(pairs), state is None...  17.6 us
  transfers between devices with their start and end apart: 58, of which 25 were waited for; matrix products, arithmetic and copies ran while one was open for 17% of the time, Pallas kernels for 14%

profile of v1, /device:TPU:0, one launch (start us, length us, event | category | flops | bytes accessed | tf_op | source)
XLA Modules:
  0.0 564.4 jit_solution(5380605668843236812)
XLA Ops:
  11.2 6.1 %concatenate.119 = bf16[576]{0:T(1024)(128)(2,1)S(1)} concatenate(bf16[48]{0:T(256)(128)(2,1)} %param.27, bf16[48]{0:T(256)(128)(2,1)} %param.28, bf16[48]{0:T(256)(128)(2,1)} %param.29, bf16[48]{0:T(256)(128)(2,1)} %param.30, bf16[48]{0:T(256)(128)(2,1)} %param.31, bf16[192]{0:T(256)(128)(2,1)} %param.32, bf16[48]{0:T(256)(128)(2,1)} %param.33, bf16[48]{0:T(256)(128)(2,1)} %param.34, ...), dimensions={0} | concatenate | bytes 2304 | tf_op jit(solution)/shard_map/concatenate | solution.py:627
  30.9 8.1 %collective-permute-done.2.refs_2_ = bf16[2,56,576]{2,1,0:T(8,128)(2,1)S(1)} collective-permute-done((bf16[2,56,576]{2,1,0:T(8,128)(2,1)S(1)}, bf16[2,56,576]{2,1,0:T(8,128)(2,1)S(1)}, u32[]{:S(2)}, u32[]{:S(2)}) %collective-permute-start.2) | collective-permute-done | bytes 129056 | tf_op jit(solution)/shard_map/ppermute | solution.py:367
  41.3 36.1 %shard_map.313 = (bf16[16,48,576]{2,1,0:T(8,128)(2,1)}, bf16[16,8,576]{2,1,0:T(8,128)(2,1)}) custom-call(s32[1]{0:T(128)} %bitcast.1.me_ref, bf16[2,56,576]{2,1,0:T(8,128)(2,1)} %copy-done.75, bf16[2,56,576]{2,1,0:T(8,128)(2,1)} %copy-done.86, bf16[2,56,576]{2,1,0:T(8,128)(2,1)} %copy-done.87, bf16[2,56,576]{2,1,0:T(8,128)(2,1)} %copy-done.88, ...), custom_call_target="tpu_custom_call" | custom-call | tf_op jit(solution)/shard_map/pallas_call | solution.py:566
  81.0 9.0 %collective-permute-done.9 = bf16[256,768]{1,0:T(8,128)(2,1)S(1)} collective-permute-done((bf16[256,768]{1,0:T(8,128)(2,1)S(1)}, bf16[256,768]{1,0:T(8,128)(2,1)S(1)}, u32[]{:S(2)}, u32[]{:S(2)}) %collective-permute-start.9) | collective-permute-done | bytes 393248 | tf_op jit(solution)/shard_map/ppermute | solution.py:367
  94.1 9.3 %collective-permute-done.10.refs_1_.refs_4_ = bf16[384,512]{1,0:T(8,128)(2,1)S(1)} collective-permute-done((bf16[384,512]{1,0:T(8,128)(2,1)S(1)}, bf16[384,512]{1,0:T(8,128)(2,1)S(1)}, u32[]{:S(2)}, u32[]{:S(2)}) %collective-permute-start.10) | collective-permute-done | bytes 393248 | tf_op jit(solution)/shard_map/ppermute | solution.py:367
  108.1 5.8 %collective-permute-done.19 = bf16[256,768]{1,0:T(8,128)(2,1)S(1)} collective-permute-done((bf16[256,768]{1,0:T(8,128)(2,1)S(1)}, bf16[256,768]{1,0:T(8,128)(2,1)S(1)}, u32[]{:S(2)}, u32[]{:S(2)}) %collective-permute-start.19) | collective-permute-done | bytes 393248 | tf_op jit(solution)/shard_map/ppermute | solution.py:367
  115.2 4.8 collective-permute-done.15
  121.2 20.5 %collective-permute-done.12 = bf16[384,512]{1,0:T(8,128)(2,1)S(1)} collective-permute-done((bf16[384,512]{1,0:T(8,128)(2,1)}, bf16[384,512]{1,0:T(8,128)(2,1)S(1)}, u32[]{:S(2)}, u32[]{:S(2)}) %collective-permute-start.12) | collective-permute-done | bytes 393248 | tf_op jit(solution)/shard_map/ppermute | solution.py:367
  142.8 3.6 shard_map.318
  150.6 3.5 shard_map.315
  154.1 3.5 shard_map.316
  157.6 3.5 shard_map.317
  163.9 5.6 %collective-permute-done.21 = bf16[384,256]{1,0:T(8,128)(2,1)} collective-permute-done((bf16[384,256]{1,0:T(8,128)(2,1)}, bf16[384,256]{1,0:T(8,128)(2,1)}, u32[]{:S(2)}, u32[]{:S(2)}) %collective-permute-start.21) | collective-permute-done | bytes 196640 | tf_op jit(solution)/shard_map/ppermute | solution.py:367
  187.8 7.6 %multiply_convert_fusion = (bf16[256,1536]{1,0:T(8,128)(2,1)}, f32[256,1536]{1,0:T(8,128)}, f32[256,1536]{1,0:T(8,128)}) fusion(f32[1536]{0:T(1024)} %add.378, bf16[256,768]{1,0:T(8,128)(2,1)} %fusion.63, bf16[1536,1536]{1,0:T(8,128)(2,1)} %all-gather.6.cloned.1.call-done), kind=kOutput, calls=%fused_computation.32 | convolution fusion | flops 629932032 | bytes 6692864 | tf_op jit(solution)/shard_map/dot_general | solution.py:32
  195.4 5.5 multiply_convert_fusion.1
  200.9 9.1 %all-gather.8.cloned.1.call-done = bf16[6144,384]{1,0:T(8,128)(2,1)} async-done(((bf16[192,384]{1,0:T(8,128)(2,1)}), bf16[6144,384]{1,0:T(8,128)(2,1)}) %all-gather.8.cloned.1.call-update) | async-done | bytes 4718608 | tf_op jit(solution)/shard_map/all_gather | solution.py:616
  253.0 4.9 collective-permute-done.23
  271.6 5.0 shard_map.319
  278.2 5.9 %shard_map.320 = (f32[192,512]{1,0:T(8,128)S(1)}, bf16[384,512]{1,0:T(8,128)(2,1)S(1)}, bf16[384,512]{1,0:T(8,128)(2,1)}) custom-call(bf16[192,512]{1,0:T(8,128)(2,1)S(1)} %fusion.38.refs_0_, bf16[192,512]{1,0:T(8,128)(2,1)S(1)} %pad_maximum_fusion.24.refs_1_, f32[3,8,512]{2,1,0:T(8,128)S(1)} %copy-done.7, f32[3,8,512]{2,1,0:T(8,128)S(1)} %broadcast_in_dim.28.refs_3_, ...), custom_call_target="tpu_custom_call" | custom-call | tf_op jit(solution)/shard_map/pallas_call | solution.py:533
  285.5 4.3 pad_maximum_fusion.1
  298.5 3.6 collective-permute-start.28
  303.9 7.9 %collective-permute-done.28 = bf16[384,512]{1,0:T(8,128)(2,1)S(1)} collective-permute-done((bf16[384,512]{1,0:T(8,128)(2,1)S(1)}, bf16[384,512]{1,0:T(8,128)(2,1)S(1)}, u32[]{:S(2)}, u32[]{:S(2)}) %collective-permute-start.28) | collective-permute-done | bytes 393248 | tf_op jit(solution)/shard_map/ppermute | solution.py:367
  312.8 5.3 collective-permute-start.31
  321.3 5.0 shard_map.323
  327.4 5.1 shard_map.321
  335.3 5.1 shard_map.322
  343.2 10.0 %collective-permute-done.33 = bf16[384,512]{1,0:T(8,128)(2,1)S(1)} collective-permute-done((bf16[384,512]{1,0:T(8,128)(2,1)S(1)}, bf16[384,512]{1,0:T(8,128)(2,1)S(1)}, u32[]{:S(2)}, u32[]{:S(2)}) %collective-permute-start.33) | collective-permute-done | bytes 393248 | tf_op jit(solution)/shard_map/ppermute | solution.py:367
  379.2 4.1 collective-permute-done.39
  384.6 4.4 collective-permute-done.41
  392.4 7.6 %collective-permute-done.36 = bf16[256,768]{1,0:T(8,128)(2,1)S(1)} collective-permute-done((bf16[256,768]{1,0:T(8,128)(2,1)S(1)}, bf16[256,768]{1,0:T(8,128)(2,1)S(1)}, u32[]{:S(2)}, u32[]{:S(2)}) %collective-permute-start.36) | collective-permute-done | bytes 393248 | tf_op jit(solution)/shard_map/ppermute | solution.py:379
  401.1 42.3 %reduce-scatter.6.cloned.1.call-done = bf16[48,1536]{1,0:T(8,128)(2,1)} async-done(((bf16[1536,1536]{1,0:T(8,128)(2,1)}), bf16[48,1536]{1,0:T(8,128)(2,1)}) %reduce-scatter.6.cloned.1.call-update) | async-done | bytes 147472 | tf_op jit(solution)/shard_map/reduce_scatter | solution.py:759
  445.0 110.7 %reduce-scatter.8.cloned.1.call-done = bf16[192,384]{1,0:T(8,128)(2,1)} async-done(((bf16[6144,384]{1,0:T(8,128)(2,1)}), bf16[192,384]{1,0:T(8,128)(2,1)}) %reduce-scatter.8.cloned.1.call-update) | async-done | bytes 147472 | tf_op jit(solution)/shard_map/reduce_scatter | solution.py:760
  (525 shorter events, 174.0 us)
Async XLA Ops:
  7.2 175.3 %all-gather.4.cloned.1.call-start = ((), (), s32[]{:S(2)}) async-start(), calls=%async_computation.3 | async-start | bytes 1216512 | tf_op jit(solution)/shard_map/all_gather | solution.py:614
  7.9 179.9 %all-gather.6.cloned.1.call-start = ((), (), s32[]{:S(2)}) async-start(), calls=%async_computation.4 | async-start | bytes 4866048 | tf_op jit(solution)/shard_map/all_gather | solution.py:615
  8.7 201.3 %all-gather.8.cloned.1.call-start = ((), (), s32[]{:S(2)}) async-start(), calls=%async_computation.5 | async-start | bytes 4866048 | tf_op jit(solution)/shard_map/all_gather | solution.py:616
  9.4 350.3 %reduce-scatter.4.cloned.1.call-start = ((), (), s32[]{:S(2)}) async-start(), calls=%async_computation.6 | async-start | bytes 1216512 | tf_op jit(solution)/shard_map/reduce_scatter | solution.py:758
  21.4 56.0 %collective-permute-start.8 = (bf16[256,768]{1,0:T(8,128)(2,1)}, bf16[256,768]{1,0:T(8,128)(2,1)S(1)}, u32[]{:S(2)}, u32[]{:S(2)}) collective-permute-start(bf16[256,768]{1,0:T(8,128)(2,1)} %bitcast.103), channel_id=1, source_target_pairs={{0,1},{1,0},{2,3},{3,2},{4,5},{5,4},{6,7},{7,6},{8,9},{9,8},{10,11... | collective-permute-start | bytes 1179656 | tf_op jit(solution)/shard_map/ppermute | solution.py:379
  25.9 13.2 %collective-permute-start.2 = (bf16[2,56,576]{2,1,0:T(8,128)(2,1)S(1)}, bf16[2,56,576]{2,1,0:T(8,128)(2,1)S(1)}, u32[]{:S(2)}, u32[]{:S(2)}) collective-permute-start(bf16[2,56,576]{2,1,0:T(8,128)(2,1)S(1)} %pad_maximum_fusion.26.refs_0_), channel_id=1, source_target_pairs={{0,16},{2,18},{4,20},{6,22},{8,24},{10,26},{12,28},{14,30},{16,0},... | collective-permute-start | bytes 387080 | tf_op jit(solution)/shard_map/ppermute | solution.py:367
  28.5 10.6 %collective-permute-start.3 = (bf16[2,56,576]{2,1,0:T(8,128)(2,1)S(1)}, bf16[2,56,576]{2,1,0:T(8,128)(2,1)S(1)}, u32[]{:S(2)}, u32[]{:S(2)}) collective-permute-start(bf16[2,56,576]{2,1,0:T(8,128)(2,1)S(1)} %pad_maximum_fusion.26.refs_0_), channel_id=1, source_target_pairs={{0,24},{2,26},{4,28},{6,30},{8,16},{10,18},{12,20},{14,22},{16,8},... | collective-permute-start | bytes 387080 | tf_op jit(solution)/shard_map/ppermute | solution.py:367
  28.5 11.7 %collective-permute-start.4 = (bf16[2,56,576]{2,1,0:T(8,128)(2,1)S(1)}, bf16[2,56,576]{2,1,0:T(8,128)(2,1)S(1)}, u32[]{:S(2)}, u32[]{:S(2)}) collective-permute-start(bf16[2,56,576]{2,1,0:T(8,128)(2,1)S(1)} %pad_maximum_fusion.26.refs_0_), channel_id=1, source_target_pairs={{0,2},{2,0},{4,6},{6,4},{8,10},{10,8},{12,14},{14,12},{16,18},{18,... | collective-permute-start | bytes 387080 | tf_op jit(solution)/shard_map/ppermute | solution.py:367
  30.9 9.3 %collective-permute-start.5 = (bf16[2,56,576]{2,1,0:T(8,128)(2,1)S(1)}, bf16[2,56,576]{2,1,0:T(8,128)(2,1)S(1)}, u32[]{:S(2)}, u32[]{:S(2)}) collective-permute-start(bf16[2,56,576]{2,1,0:T(8,128)(2,1)S(1)} %collective-permute-done.1.refs_1_), channel_id=1, source_target_pairs={{0,2},{2,0},{4,6},{6,4},{8,10},{10,8},{12,14},{14,12},{16,18},{18,... | collective-permute-start | bytes 387080 | tf_op jit(solution)/shard_map/ppermute | solution.py:367
  77.5 12.4 %collective-permute-start.9 = (bf16[256,768]{1,0:T(8,128)(2,1)S(1)}, bf16[256,768]{1,0:T(8,128)(2,1)S(1)}, u32[]{:S(2)}, u32[]{:S(2)}) collective-permute-start(bf16[256,768]{1,0:T(8,128)(2,1)S(1)} %get-tuple-element.118), channel_id=1, source_target_pairs={{0,4},{2,6},{4,0},{6,2},{8,12},{10,14},{12,8},{14,10},{16,20},{18,... | collective-permute-start | bytes 1179656 | tf_op jit(solution)/shard_map/ppermute | solution.py:367
  90.8 12.5 %collective-permute-start.10 = (bf16[384,512]{1,0:T(8,128)(2,1)S(1)}, bf16[384,512]{1,0:T(8,128)(2,1)S(1)}, u32[]{:S(2)}, u32[]{:S(2)}) collective-permute-start(bf16[384,512]{1,0:T(8,128)(2,1)S(1)} %fusion.31.refs_1_.refs_4_), channel_id=1, source_target_pairs={{0,8},{2,10},{4,12},{6,14},{8,0},{10,2},{12,4},{14,6},{16,24},{18,... | collective-permute-start | bytes 1179656 | tf_op jit(solution)/shard_map/ppermute | solution.py:367
  92.6 12.7 %collective-permute-start.13 = (bf16[384,512]{1,0:T(8,128)(2,1)S(1)}, bf16[384,512]{1,0:T(8,128)(2,1)}, u32[]{:S(2)}, u32[]{:S(2)}) collective-permute-start(bf16[384,512]{1,0:T(8,128)(2,1)S(1)} %fusion.31.refs_1_.refs_4_), channel_id=1, source_target_pairs={{8,16},{10,18},{12,20},{14,22},{16,8},{18,10},{20,12},{22,14},{9,1... | collective-permute-start | bytes 1179656 | tf_op jit(solution)/shard_map/ppermute | solution.py:367
  105.3 14.8 %collective-permute-start.15 = (bf16[384,512]{1,0:T(8,128)(2,1)}, bf16[384,512]{1,0:T(8,128)(2,1)}, u32[]{:S(2)}, u32[]{:S(2)}) collective-permute-start(bf16[384,512]{1,0:T(8,128)(2,1)} %collective-permute-done.13), channel_id=1, source_target_pairs={{8,0},{10,2},{12,4},{14,6},{16,24},{18,26},{20,28},{22,30},{9,1},{... | collective-permute-start | bytes 1179656 | tf_op jit(solution)/shard_map/ppermute | solution.py:367
  106.8 40.4 %collective-permute-start.18 = (bf16[384,512]{1,0:T(8,128)(2,1)S(1)}, bf16[384,512]{1,0:T(8,128)(2,1)S(1)}, u32[]{:S(2)}, u32[]{:S(2)}) collective-permute-start(bf16[384,512]{1,0:T(8,128)(2,1)S(1)} %fusion.31.refs_1_.refs_4_), channel_id=1, source_target_pairs={{0,2},{2,0},{4,6},{6,4},{8,10},{10,8},{12,14},{14,12},{16,18},{18,... | collective-permute-start | bytes 1179656 | tf_op jit(solution)/shard_map/ppermute | solution.py:367
  106.8 34.9 %collective-permute-start.12 = (bf16[384,512]{1,0:T(8,128)(2,1)}, bf16[384,512]{1,0:T(8,128)(2,1)S(1)}, u32[]{:S(2)}, u32[]{:S(2)}) collective-permute-start(bf16[384,512]{1,0:T(8,128)(2,1)} %collective-permute-done.11), channel_id=1, source_target_pairs={{8,0},{10,2},{12,4},{14,6},{16,24},{18,26},{20,28},{22,30},{9,1},{... | collective-permute-start | bytes 1179656 | tf_op jit(solution)/shard_map/ppermute | solution.py:367
  114.7 28.1 %collective-permute-start.20 = (bf16[384,512]{1,0:T(8,128)(2,1)S(1)}, bf16[384,512]{1,0:T(8,128)(2,1)S(1)}, u32[]{:S(2)}, u32[]{:S(2)}) collective-permute-start(bf16[384,512]{1,0:T(8,128)(2,1)S(1)} %fusion.32.refs_2_.refs_5_), channel_id=1, source_target_pairs={{0,2},{2,0},{4,6},{6,4},{8,10},{10,8},{12,14},{14,12},{16,18},{18,... | collective-permute-start | bytes 1179656 | tf_op jit(solution)/shard_map/ppermute | solution.py:367
  114.8 35.8 %collective-permute-start.17 = (bf16[384,512]{1,0:T(8,128)(2,1)S(1)}, bf16[384,512]{1,0:T(8,128)(2,1)S(1)}, u32[]{:S(2)}, u32[]{:S(2)}) collective-permute-start(bf16[384,512]{1,0:T(8,128)(2,1)S(1)} %collective-permute-done.10.refs_1_.refs_4_), channel_id=1, source_target_pairs={{0,2},{2,0},{4,6},{6,4},{8,10},{10,8},{12,14},{14,12},{16,18},{18,... | collective-permute-start | bytes 1179656 | tf_op jit(solution)/shard_map/ppermute | solution.py:367
  121.1 33.0 %collective-permute-start.16 = (bf16[384,512]{1,0:T(8,128)(2,1)S(1)}, bf16[384,512]{1,0:T(8,128)(2,1)S(1)}, u32[]{:S(2)}, u32[]{:S(2)}) collective-permute-start(bf16[384,512]{1,0:T(8,128)(2,1)S(1)} %broadcast_select_fusion.refs_1_.refs_4_), channel_id=1, source_target_pairs={{0,2},{2,0},{4,6},{6,4},{8,10},{10,8},{12,14},{14,12},{16,18},{18,... | collective-permute-start | bytes 1179656 | tf_op jit(solution)/shard_map/ppermute | solution.py:367
  141.7 15.9 %collective-permute-start.14 = (bf16[384,512]{1,0:T(8,128)(2,1)S(1)}, bf16[384,512]{1,0:T(8,128)(2,1)S(1)}, u32[]{:S(2)}, u32[]{:S(2)}) collective-permute-start(bf16[384,512]{1,0:T(8,128)(2,1)S(1)} %broadcast_select_fusion.1.refs_1_.refs_4_), channel_id=1, source_target_pairs={{0,2},{2,0},{4,6},{6,4},{8,10},{10,8},{12,14},{14,12},{16,18},{18,... | collective-permute-start | bytes 1179656 | tf_op jit(solution)/shard_map/ppermute | solution.py:367
  171.3 9.3 %collective-permute-start.22 = (bf16[384,256]{1,0:T(8,128)(2,1)S(1)}, bf16[384,256]{1,0:T(8,128)(2,1)}, u32[]{:S(2)}, u32[]{:S(2)}) collective-permute-start(bf16[384,256]{1,0:T(8,128)(2,1)S(1)} %broadcast_select_fusion.6), channel_id=1, source_target_pairs={{0,1},{1,0},{2,3},{3,2},{4,5},{5,4},{6,7},{7,6},{8,9},{9,8},{10,11... | collective-permute-start | bytes 589832 | tf_op jit(solution)/shard_map/ppermute | solution.py:379
  232.1 211.2 %reduce-scatter.6.cloned.1.call-start = ((), (), s32[]{:S(2)}) async-start(), calls=%async_computation.7 | async-start | bytes 4866048 | tf_op jit(solution)/shard_map/reduce_scatter | solution.py:759
  237.7 318.0 %reduce-scatter.8.cloned.1.call-start = ((), (), s32[]{:S(2)}) async-start(), calls=%async_computation.8 | async-start | bytes 4866048 | tf_op jit(solution)/shard_map/reduce_scatter | solution.py:760
  260.9 29.1 %collective-permute-start.49 = (f32[64,128]{1,0:T(8,128)}, f32[64,128]{1,0:T(8,128)}, u32[]{:S(2)}, u32[]{:S(2)}) collective-permute-start(f32[64,128]{1,0:T(8,128)} %fusion.130), channel_id=1, source_target_pairs={{0,8},{2,10},{4,12},{6,14},{8,0},{10,2},{12,4},{14,6},{16,24},{18,... | collective-permute-start | bytes 98312 | tf_op jit(solution)/shard_map/ppermute | solution.py:367
  285.5 11.7 %collective-permute-start.27 = (bf16[384,512]{1,0:T(8,128)(2,1)}, bf16[384,512]{1,0:T(8,128)(2,1)}, u32[]{:S(2)}, u32[]{:S(2)}) collective-permute-start(bf16[384,512]{1,0:T(8,128)(2,1)} %get-tuple-element.71), channel_id=1, source_target_pairs={{0,2},{2,0},{4,6},{6,4},{8,10},{10,8},{12,14},{14,12},{16,18},{18,... | collective-permute-start | bytes 1179656 | tf_op jit(solution)/shard_map/ppermute | solution.py:367
  298.5 13.3 %collective-permute-start.28 = (bf16[384,512]{1,0:T(8,128)(2,1)S(1)}, bf16[384,512]{1,0:T(8,128)(2,1)S(1)}, u32[]{:S(2)}, u32[]{:S(2)}) collective-permute-start(bf16[384,512]{1,0:T(8,128)(2,1)S(1)} %add_convert_fusion.11), channel_id=1, source_target_pairs={{0,8},{2,10},{4,12},{6,14},{24,16},{26,18},{28,20},{30,22},{1,9},{... | collective-permute-start | bytes 1179656 | tf_op jit(solution)/shard_map/ppermute | solution.py:367
  312.8 20.2 %collective-permute-start.31 = (bf16[384,512]{1,0:T(8,128)(2,1)}, bf16[384,512]{1,0:T(8,128)(2,1)}, u32[]{:S(2)}, u32[]{:S(2)}) collective-permute-start(bf16[384,512]{1,0:T(8,128)(2,1)} %get-tuple-element.103), channel_id=1, source_target_pairs={{0,8},{2,10},{4,12},{6,14},{24,16},{26,18},{28,20},{30,22},{1,9},{... | collective-permute-start | bytes 1179656 | tf_op jit(solution)/shard_map/ppermute | solution.py:367
  326.3 16.0 %collective-permute-start.34 = (bf16[384,512]{1,0:T(8,128)(2,1)S(1)}, bf16[384,512]{1,0:T(8,128)(2,1)S(1)}, u32[]{:S(2)}, u32[]{:S(2)}) collective-permute-start(bf16[384,512]{1,0:T(8,128)(2,1)S(1)} %get-tuple-element.77), channel_id=1, source_target_pairs={{0,2},{2,0},{4,6},{6,4},{8,10},{10,8},{12,14},{14,12},{16,18},{18,... | collective-permute-start | bytes 1179656 | tf_op jit(solution)/shard_map/ppermute | solution.py:367
  341.6 11.6 %collective-permute-start.33 = (bf16[384,512]{1,0:T(8,128)(2,1)S(1)}, bf16[384,512]{1,0:T(8,128)(2,1)S(1)}, u32[]{:S(2)}, u32[]{:S(2)}) collective-permute-start(bf16[384,512]{1,0:T(8,128)(2,1)S(1)} %add_convert_fusion.6), channel_id=1, source_target_pairs={{0,8},{2,10},{4,12},{6,14},{8,0},{10,2},{12,4},{14,6},{16,24},{18,... | collective-permute-start | bytes 1179656 | tf_op jit(solution)/shard_map/ppermute | solution.py:367
  356.0 14.8 %collective-permute-start.37 = (bf16[4,2,48,576]{3,2,1,0:T(8,128)(2,1)}, bf16[4,2,48,576]{3,2,1,0:T(8,128)(2,1)}, u32[]{:S(2)}, u32[]{:S(2)}) collective-permute-start(bf16[4,2,48,576]{3,2,1,0:T(8,128)(2,1)} %select_bitcast_fusion), channel_id=1, source_target_pairs={{0,2},{2,0},{4,6},{6,4},{8,10},{10,8},{12,14},{14,12},{16,18},{18,... | collective-permute-start | bytes 1327112 | tf_op jit(solution)/shard_map/ppermute | solution.py:367
  365.4 23.7 %collective-permute-start.35 = (bf16[512,768]{1,0:T(8,128)(2,1)S(1)}, bf16[512,768]{1,0:T(8,128)(2,1)S(1)}, u32[]{:S(2)}, u32[]{:S(2)}) collective-permute-start(bf16[512,768]{1,0:T(8,128)(2,1)S(1)} %pad_maximum_fusion.6), channel_id=1, source_target_pairs={{0,4},{2,6},{4,0},{6,2},{8,12},{10,14},{12,8},{14,10},{16,20},{18,... | collective-permute-start | bytes 2359304 | tf_op jit(solution)/shard_map/ppermute | solution.py:367
  372.8 10.6 %collective-permute-start.39 = (bf16[2,48,576]{2,1,0:T(8,128)(2,1)S(1)}, bf16[2,48,576]{2,1,0:T(8,128)(2,1)S(1)}, u32[]{:S(2)}, u32[]{:S(2)}) collective-permute-start(bf16[2,48,576]{2,1,0:T(8,128)(2,1)S(1)} %get-tuple-element.126), channel_id=1, source_target_pairs={{0,16},{2,18},{4,20},{6,22},{8,24},{10,26},{12,28},{14,30},{16,0},... | collective-permute-start | bytes 331784 | tf_op jit(solution)/shard_map/ppermute | solution.py:367
  389.6 10.4 %collective-permute-start.36 = (bf16[256,768]{1,0:T(8,128)(2,1)S(1)}, bf16[256,768]{1,0:T(8,128)(2,1)S(1)}, u32[]{:S(2)}, u32[]{:S(2)}) collective-permute-start(bf16[256,768]{1,0:T(8,128)(2,1)S(1)} %select_convert_fusion), channel_id=1, source_target_pairs={{0,1},{1,0},{2,3},{3,2},{4,5},{5,4},{6,7},{7,6},{8,9},{9,8},{10,11... | collective-permute-start | bytes 1179656 | tf_op jit(solution)/shard_map/ppermute | solution.py:379
  (160 other events, 971.8 us)
Sparse Core Ops, SparseCore 0:
  10.9 61.6 all-gather.3
  75.5 66.0 all-gather.5
  144.5 65.4 all-gather.7
  232.2 95.4 reduce-scatter.3
  333.1 110.1 reduce-scatter.5
  449.5 106.1 reduce-scatter.7
